TPU v7x, 32 devices: a whole 2x2x4 slice. The times are simulated.
32 devices in a mesh: pipe: 4 (over z), seq: 4 (over y, x), exp: 2 (over core).
Axes of the slice: x: 2, y: 2, z: 4, core: 2. Of those that a mesh axis runs over, the one named last changes fastest.
Arguments:
- queries: bfloat16 [4, 2, 512, 4096], P('pipe', 'exp', 'seq'), may hold values from -160 to 160
- key_rows: bfloat16 [4, 2, 512, 256], P('pipe', 'exp', 'seq'), may hold values from -160 to 160
- value_rows: bfloat16 [4, 2, 512, 256], P('pipe', 'exp', 'seq'), may hold values from -6 to 6
- residual: bfloat16 [4, 2, 512, 4096], P('pipe', 'exp', 'seq'), may hold values from -6 to 6
- doc_lengths: int32 [4, 2, 8], P('pipe', 'exp'), may hold values from 1 to 128, 512 in all within a row
- norm_gain: float32 [4, 4096], P('pipe'), may hold values from 0.1 to 1.9
- kv_weight: bfloat16 [4, 4096, 512], P('pipe', ('seq', 'exp')), may hold values from -0.09375 to 0.09375
Outputs:
- context: bfloat16 [4, 2, 512, 4096], P('pipe', 'exp', 'seq')
- kv_next: bfloat16 [4, 2, 512, 512], P('pipe', 'exp', 'seq')
Inputs may be any that keep to these rules, and one draw needn't show every extreme that they name: `doc_lengths`: every pack has a document of exactly 128 tokens and none longer.
All inputs are finite; a program needn't handle non-finite values.
Results may differ from a plain program's by a relative error of at most 0.0058.
Values may be sent and summed in bfloat16 or wider, within the bound.
No kernel may reach another device: no remote copies, remote signals or barrier semaphores. Data moves between devices by JAX's collectives and lax.ppermute only.
A program may use at most 64 MiB of HBM per device.

v0:
```python
import functools
import math

import jax
import jax.numpy as jnp
from jax import lax
from jax.experimental import pallas as pl
from jax.experimental.pallas import tpu as pltpu
from jax.sharding import PartitionSpec as P


DH = 128


epsilon = 1e-06
MASKED = -1e30

WHOLE = pl.BlockSpec(memory_space=pltpu.VMEM)
FAR = pl.BlockSpec(memory_space=pltpu.HBM)


def near(array):
    return pltpu.with_memory_space_constraint(array, pltpu.VMEM)


def far(array):
    return pltpu.with_memory_space_constraint(array, pltpu.HBM)


def budget(mebibytes):
    return pltpu.CompilerParams(vmem_limit_bytes=mebibytes << 20)


def shifted(block, distance):
    devices = range(lax.axis_size("pipe"))
    route = [(i - distance, i) for i in devices if i - distance in devices]
    return lax.ppermute(block, "pipe", route)


def exchanged(block, axis, bit):
    return lax.ppermute(block, axis, [(i, i ^ bit) for i in range(lax.axis_size(axis))])


def run_copies(copies):
    for copy in copies:
        copy.start()
    for copy in copies:
        copy.wait()


def prepare_kernel(key_ref, value_ref, gain_ref, weight_ref, pair_ref, *refs):
    piece_refs, (weight, gain, sems) = refs[:-3], refs[-3:]
    width = key_ref.shape[1]
    depth = weight_ref.shape[0]
    at = (lax.axis_index("seq") * lax.axis_size("exp") + lax.axis_index("exp")) * depth
    run_copies(
        [
            pltpu.make_async_copy(weight_ref, weight, sems.at[0]),
            pltpu.make_async_copy(gain_ref, gain, sems.at[1]),
            pltpu.make_async_copy(key_ref, pair_ref.at[:, :width], sems.at[2]),
            pltpu.make_async_copy(value_ref, pair_ref.at[:, width:], sems.at[3]),
        ]
    )
    if depth % DH:
        wide = gain[...]
        place = lax.broadcasted_iota(jnp.int32, (depth, wide.shape[1]), 0) + at
        here = place == lax.broadcasted_iota(jnp.int32, place.shape, 1)
        column = jnp.sum(jnp.where(here, wide, 0.0), axis=1, keepdims=True)
    else:
        wide = gain[:, pl.ds(pl.multiple_of(at, depth), depth)]
        column = jnp.transpose(jnp.broadcast_to(wide, (DH, depth)))
    rows = depth // len(piece_refs)
    for index, piece_ref in enumerate(piece_refs):
        part = slice(index * rows, (index + 1) * rows)
        for left in range(0, weight.shape[1], DH):
            cols = slice(left, left + DH)
            piece_ref[:, cols] = (weight[part, cols].astype(jnp.float32) * column[part]).astype(jnp.bfloat16)


def prepare(key_rows, value_rows, norm_gain, weight, pieces):
    rows, width = key_rows.shape
    depth, cols = weight.shape
    piece = pltpu.VMEM((depth // pieces, cols), weight.dtype)
    return pl.pallas_call(
        prepare_kernel,
        out_shape=(pltpu.VMEM((rows, 2 * width), key_rows.dtype), *[piece] * pieces),
        in_specs=[FAR] * 4,
        out_specs=(WHOLE,) * (1 + pieces),
        scratch_shapes=[
            pltpu.VMEM((depth, cols), weight.dtype),
            pltpu.VMEM(norm_gain.shape, jnp.float32),
            pltpu.SemaphoreType.DMA((4,)),
        ],
        compiler_params=budget(6),
        name="prepare",
    )(*[far(array) for array in (key_rows, value_rows, norm_gain, weight)])


def fetch_kernel(*refs):
    count = (len(refs) - 1) // 2
    sems = refs[-1]
    run_copies(
        [pltpu.make_async_copy(refs[i], refs[count + i], sems.at[i]) for i in range(count)]
    )


def fetch(*arrays):
    return pl.pallas_call(
        fetch_kernel,
        out_shape=tuple(pltpu.VMEM(array.shape, array.dtype) for array in arrays),
        in_specs=[FAR] * len(arrays),
        out_specs=(WHOLE,) * len(arrays),
        scratch_shapes=[pltpu.SemaphoreType.DMA((len(arrays),))],
        compiler_params=budget(4),
        name="fetch",
    )(*[far(array) for array in arrays])


def attend_kernel(groups, longest, score_scale, far_lengths_ref, query_ref, residual_ref, *refs):
    pair_refs, (context_ref, layer_ref, inverse_ref, every, lengths_ref, sem) = refs[:-6], refs[-6:]
    lengths_copy = pltpu.make_async_copy(far_lengths_ref, lengths_ref, sem)
    lengths_copy.start()
    tok_rows, row_width = query_ref.shape
    half_rows = tok_rows // 2
    kv_width = every.shape[2] // 2
    kv_heads = kv_width // DH
    per_kv = row_width // DH // kv_heads
    window = longest + half_rows
    blocks = window // half_rows
    own = lax.axis_index("seq")
    if len(pair_refs) == 1:
        every[...] = pair_refs[0][...].reshape(every.shape)
    else:
        for bit, pair_ref in enumerate(pair_refs):
            every[own ^ bit] = pair_ref[...]
    lengths_copy.wait()
    bounds = []
    total = jnp.int32(0)
    for doc in range(lengths_ref.shape[1]):
        total = total + lengths_ref[0, doc]
        bounds.append(total)
    exponent = score_scale * math.log2(math.e)
    for run in range(2):
        block = own if run == 0 else 2 * groups - 1 - own
        first_pos = block * half_rows
        rows = slice(run * half_rows, (run + 1) * half_rows)
        query_pos = first_pos + lax.broadcasted_iota(jnp.int32, (half_rows, window), 0)
        key_pos = first_pos + half_rows - window + lax.broadcasted_iota(jnp.int32, (half_rows, window), 1)
        doc_start = jnp.zeros((half_rows, window), jnp.int32)
        for bound in bounds:
            doc_start = jnp.where(bound <= query_pos, bound, doc_start)
        visible = (doc_start <= key_pos) & (key_pos <= query_pos)
        key_parts, value_parts = [], []
        for back in range(blocks - 1, -1, -1):
            natural = jnp.maximum(block - back, 0)
            second = natural >= groups
            owner = jnp.where(second, 2 * groups - 1 - natural, natural)
            offset = jnp.where(second, half_rows, 0)
            part = every[owner, pl.ds(pl.multiple_of(offset, half_rows), half_rows), :]
            key_parts.append(part[:, :kv_width])
            value_parts.append(part[:, kv_width:])
        key_win = jnp.concatenate(key_parts, axis=0)
        value_win = jnp.concatenate(value_parts, axis=0)
        squares = jnp.zeros((half_rows, DH), jnp.float32)
        for group in range(kv_heads):
            lanes = slice(group * DH, (group + 1) * DH)
            query_stack = jnp.concatenate(
                [
                    query_ref[rows, (group * per_kv + h) * DH : (group * per_kv + h + 1) * DH]
                    for h in range(per_kv)
                ],
                axis=0,
            )
            scores = lax.dot_general(
                query_stack, key_win[:, lanes], (((1,), (1,)), ((), ())), preferred_element_type=jnp.float32
            )
            masked = jnp.where(visible[None], scores.reshape(per_kv, half_rows, window), MASKED)
            row_max = jnp.max(masked, axis=2, keepdims=True)
            weights = jnp.exp2((masked - row_max) * exponent)
            sums = jnp.sum(weights, axis=2, keepdims=True)
            rounded = weights.astype(jnp.bfloat16).reshape(per_kv * half_rows, window)
            mixed = jnp.dot(rounded, value_win[:, lanes], preferred_element_type=jnp.float32)
            context = (mixed.reshape(per_kv, half_rows, DH) / sums).astype(jnp.bfloat16)
            for h in range(per_kv):
                cols = slice((group * per_kv + h) * DH, (group * per_kv + h + 1) * DH)
                context_ref[rows, cols] = context[h]
                added = (
                    residual_ref[rows, cols].astype(jnp.float32) + context[h].astype(jnp.float32)
                ).astype(jnp.bfloat16)
                layer_ref[rows, cols] = added
                wide = added.astype(jnp.float32)
                squares = squares + wide * wide
        mean_square = jnp.sum(squares, axis=1, keepdims=True) * (1.0 / row_width)
        inverse_ref[rows, :] = jnp.broadcast_to(lax.rsqrt(mean_square + epsilon), (half_rows, DH))


def attend(lengths, queries, residual, pairs, groups):
    tok_rows, _ = queries.shape
    longest = tok_rows * groups // 4
    pair_width = pairs[0].shape[1]
    shape = pltpu.VMEM(queries.shape, jnp.bfloat16)
    return pl.pallas_call(
        functools.partial(attend_kernel, groups, longest, 1.0 / math.sqrt(DH)),
        out_shape=(shape, shape, pltpu.VMEM((tok_rows, DH), jnp.float32)),
        in_specs=[FAR] + [WHOLE] * (2 + len(pairs)),
        out_specs=(WHOLE,) * 3,
        scratch_shapes=[
            pltpu.VMEM((groups, tok_rows, pair_width), jnp.bfloat16),
            pltpu.SMEM(lengths.shape, jnp.int32),
            pltpu.SemaphoreType.DMA,
        ],
        compiler_params=budget(16),
        name="attend",
    )(far(lengths), *[near(array) for array in (queries, residual, *pairs)])


def project_kernel(places, last, layer_ref, *refs):
    piece_refs = refs[: len(places)]
    rest = refs[len(places) :]
    out_ref = rest[-1]
    depth = layer_ref.shape[1] // (lax.axis_size("seq") * lax.axis_size("exp"))
    seq, core = lax.axis_index("seq"), lax.axis_index("exp")
    total = None if len(rest) == 1 else rest[0][...]
    for (bit, kind, first), piece_ref in zip(places, piece_refs):
        rows = piece_ref.shape[0]
        column = ((seq ^ bit) * 2 + (core ^ kind)) * depth + first
        part = jnp.dot(
            layer_ref[:, pl.ds(pl.multiple_of(column, DH), rows)], piece_ref[...], preferred_element_type=jnp.float32
        )
        total = part if total is None else total + part
    if last:
        inverse_ref = rest[1]
        for left in range(0, total.shape[1], DH):
            cols = slice(left, left + DH)
            out_ref[:, cols] = (total[:, cols] * inverse_ref[...]).astype(jnp.bfloat16)
    else:
        out_ref[...] = total


def project(layer, held, so_far=None, inverse=None):
    places = tuple(held)
    last = inverse is not None
    blocks = [held[place] for place in places]
    extra = [array for array in (so_far, inverse) if array is not None]
    shape = (layer.shape[0], blocks[0].shape[1])
    return pl.pallas_call(
        functools.partial(project_kernel, places, last),
        out_shape=pltpu.VMEM(shape, jnp.bfloat16 if last else jnp.float32),
        in_specs=[WHOLE] * (1 + len(blocks) + len(extra)),
        out_specs=WHOLE,
        compiler_params=budget(8),
        name="project",
    )(*[near(array) for array in (layer, *blocks, *extra)])


def square_of_chips(queries, key_rows, value_rows, residual, lengths, norm_gain, weight):
    pair, *parts = prepare(key_rows, value_rows, norm_gain, weight, 2)
    early, late = {}, {}

    def hold(held, bit, first, block):
        held[bit, 0, first] = block
        held[bit, 1, first] = exchanged(block, "exp", 1)

    first = 0
    for index, part in enumerate(parts):
        block = shifted(part, -1)
        hold(early, 0, first, block)
        sides = {}
        for bit in (1, 2):
            sides[bit] = exchanged(block, "seq", bit)
            hold(early, bit, first, sides[bit])
        half = block.shape[0] // 2
        for bit in (1, 2):
            start = (bit - 1) * half
            corner = exchanged(sides[bit][start : start + half], "seq", 3 - bit)
            hold(early if index == 0 else late, 3, first + start, corner)
        first += block.shape[0]
    pairs = [pair]
    for bit in (1, 2, 3):
        pairs.append(exchanged(pair, "seq", bit))
    queries, residual = fetch(queries, residual)
    context, layer, inverse = attend(lengths, queries, residual, pairs, lax.axis_size("seq"))
    so_far = project(layer, early)
    projected = project(layer, late, so_far, inverse)
    return context, shifted(projected, 1)


def any_mesh(queries, key_rows, value_rows, residual, lengths, norm_gain, weight):
    pair, part = prepare(key_rows, value_rows, norm_gain, weight, 1)
    pairs = [lax.all_gather(pair, "seq", axis=0, tiled=True)]
    context, layer, inverse = attend(lengths, queries, residual, pairs, lax.axis_size("seq"))
    every = lax.all_gather(shifted(part, -1), ("seq", "exp"), axis=0, tiled=True)
    total = jnp.dot(layer, every, preferred_element_type=jnp.float32)
    return context, shifted((total * inverse[:, :1]).astype(jnp.bfloat16), 1)


def is_square(sizes):
    return sizes["seq"] == 4 and sizes["exp"] == 2


def on_device(queries, key_rows, value_rows, residual, doc_lengths, norm_gain, kv_weight):
    square = is_square({axis: lax.axis_size(axis) for axis in ("seq", "exp")})
    context, kv_next = (square_of_chips if square else any_mesh)(
        queries[0, 0], key_rows[0, 0], value_rows[0, 0], residual[0, 0], doc_lengths[0], norm_gain, kv_weight[0]
    )
    return context[None, None], kv_next[None, None]


def solution(mesh):
    rows = P("pipe", "exp", "seq", None)
    return jax.shard_map(
        on_device,
        mesh=mesh,
        in_specs=(rows, rows, rows, rows, P("pipe", "exp", None), P("pipe", None), P("pipe", ("seq", "exp"), None)),
        out_specs=(rows, rows),
        check_vma=False,
    )
```

profile of v0, /device:TPU:0, one launch (start us, length us, event | category | flops | bytes accessed | tf_op | source)
XLA Modules:
  0.0 59.0 jit_solution(12968759834959247234)
XLA Ops:
  0.6 1.2 %prepare.1 = (bf16[128,512]{1,0:T(8,128)(2,1)S(1)}, bf16[256,512]{1,0:T(8,128)(2,1)S(1)}, bf16[256,512]{1,0:T(8,128)(2,1)S(1)}) custom-call(bf16[128,256]{1,0:T(8,128)(2,1)} %bitcast.13, bf16[128,256]{1,0:T(8,128)(2,1)} %bitcast.14, f32[1,4096]{1,0:T(1,128)} %gain_ref.1, bf16[512,512]{1,0:T(8,128)(2,1)} %bitcast.11), custom_call_target="tpu_custom_call" | custom-call | tf_op jit(solution)/shard_map/prepare/pallas_call | solution.py:84
  1.9 1.3 %collective-permute-start.10 = (bf16[256,512]{1,0:T(8,128)(2,1)S(1)}, bf16[256,512]{1,0:T(8,128)(2,1)S(1)}, u32[]{:S(2)}, u32[]{:S(2)}) collective-permute-start(bf16[256,512]{1,0:T(8,128)(2,1)S(1)} %get-tuple-element.16), channel_id=1, source_target_pairs={{8,0},{16,8},{24,16},{9,1},{17,9},{25,17},{10,2},{18,10},{26,18},{... | collective-permute-start | bytes 786440 | tf_op jit(solution)/shard_map/ppermute | solution.py:37
  3.2 1.3 %collective-permute-start.3 = (bf16[256,512]{1,0:T(8,128)(2,1)S(1)}, bf16[256,512]{1,0:T(8,128)(2,1)S(1)}, u32[]{:S(2)}, u32[]{:S(2)}) collective-permute-start(bf16[256,512]{1,0:T(8,128)(2,1)S(1)} %get-tuple-element.15), channel_id=1, source_target_pairs={{8,0},{16,8},{24,16},{9,1},{17,9},{25,17},{10,2},{18,10},{26,18},{... | collective-permute-start | bytes 786440 | tf_op jit(solution)/shard_map/ppermute | solution.py:37
  4.5 9.5 %collective-permute-done.10.refs_0_ = bf16[256,512]{1,0:T(8,128)(2,1)S(1)} collective-permute-done((bf16[256,512]{1,0:T(8,128)(2,1)S(1)}, bf16[256,512]{1,0:T(8,128)(2,1)S(1)}, u32[]{:S(2)}, u32[]{:S(2)}) %collective-permute-start.10) | collective-permute-done | bytes 262176 | tf_op jit(solution)/shard_map/ppermute | solution.py:37
  14.0 1.9 %collective-permute-start.12 = (bf16[256,512]{1,0:T(8,128)(2,1)S(1)}, bf16[256,512]{1,0:T(8,128)(2,1)S(1)}, u32[]{:S(2)}, u32[]{:S(2)}) collective-permute-start(bf16[256,512]{1,0:T(8,128)(2,1)S(1)} %collective-permute-done.10.refs_0_), channel_id=1, source_target_pairs={{0,2},{2,0},{4,6},{6,4},{1,3},{3,1},{5,7},{7,5},{8,10},{10,8},{12,... | collective-permute-start | bytes 786440 | tf_op jit(solution)/shard_map/ppermute | solution.py:41
  15.9 1.5 %collective-permute-start.14 = (bf16[256,512]{1,0:T(8,128)(2,1)S(1)}, bf16[256,512]{1,0:T(8,128)(2,1)S(1)}, u32[]{:S(2)}, u32[]{:S(2)}) collective-permute-start(bf16[256,512]{1,0:T(8,128)(2,1)S(1)} %collective-permute-done.10.refs_0_), channel_id=1, source_target_pairs={{0,4},{2,6},{4,0},{6,2},{1,5},{3,7},{5,1},{7,3},{8,12},{10,14},{12... | collective-permute-start | bytes 786440 | tf_op jit(solution)/shard_map/ppermute | solution.py:41
  17.4 0.5 collective-permute-start
  18.0 0.1 collective-permute-start.1
  18.0 0.7 %collective-permute-done.3.refs_10_ = bf16[256,512]{1,0:T(8,128)(2,1)S(1)} collective-permute-done((bf16[256,512]{1,0:T(8,128)(2,1)S(1)}, bf16[256,512]{1,0:T(8,128)(2,1)S(1)}, u32[]{:S(2)}, u32[]{:S(2)}) %collective-permute-start.3) | collective-permute-done | bytes 262176 | tf_op jit(solution)/shard_map/ppermute | solution.py:37
  18.8 1.6 %collective-permute-start.4 = (bf16[256,512]{1,0:T(8,128)(2,1)S(1)}, bf16[256,512]{1,0:T(8,128)(2,1)S(1)}, u32[]{:S(2)}, u32[]{:S(2)}) collective-permute-start(bf16[256,512]{1,0:T(8,128)(2,1)S(1)} %collective-permute-done.3.refs_10_), channel_id=1, source_target_pairs={{0,2},{2,0},{4,6},{6,4},{1,3},{3,1},{5,7},{7,5},{8,10},{10,8},{12,... | collective-permute-start | bytes 786440 | tf_op jit(solution)/shard_map/ppermute | solution.py:41
  20.4 5.6 %collective-permute-done.refs_1_ = bf16[128,512]{1,0:T(8,128)(2,1)S(1)} collective-permute-done((bf16[128,512]{1,0:T(8,128)(2,1)S(1)}, bf16[128,512]{1,0:T(8,128)(2,1)S(1)}, u32[]{:S(2)}, u32[]{:S(2)}) %collective-permute-start) | collective-permute-done | bytes 131104 | tf_op jit(solution)/shard_map/ppermute | solution.py:41
  26.0 1.6 %collective-permute-start.7 = (bf16[256,512]{1,0:T(8,128)(2,1)S(1)}, bf16[256,512]{1,0:T(8,128)(2,1)S(1)}, u32[]{:S(2)}, u32[]{:S(2)}) collective-permute-start(bf16[256,512]{1,0:T(8,128)(2,1)S(1)} %collective-permute-done.3.refs_10_), channel_id=1, source_target_pairs={{0,4},{2,6},{4,0},{6,2},{1,5},{3,7},{5,1},{7,3},{8,12},{10,14},{12... | collective-permute-start | bytes 786440 | tf_op jit(solution)/shard_map/ppermute | solution.py:41
  27.6 0.0 collective-permute-done.1.refs_2_
  27.6 0.0 collective-permute-start.11
  27.6 0.0 collective-permute-done.12.refs_2_
  27.6 0.5 collective-permute-start.20
  28.1 0.0 collective-permute-done.14.refs_4_
  28.1 1.4 %collective-permute-start.2 = (bf16[128,512]{1,0:T(8,128)(2,1)S(1)}, bf16[128,512]{1,0:T(8,128)(2,1)S(1)}, u32[]{:S(2)}, u32[]{:S(2)}) collective-permute-start(bf16[128,512]{1,0:T(8,128)(2,1)S(1)} %get-tuple-element.12.refs_0_), channel_id=1, source_target_pairs={{0,6},{2,4},{4,2},{6,0},{1,7},{3,5},{5,3},{7,1},{8,14},{10,12},{12... | collective-permute-start | bytes 393224 | tf_op jit(solution)/shard_map/ppermute | solution.py:41
  29.6 0.0 collective-permute-done.4.refs_12_
  29.6 1.6 %collective-permute-start.16 = (bf16[128,512]{1,0:T(8,128)(2,1)S(1)}, bf16[128,512]{1,0:T(8,128)(2,1)S(1)}, u32[]{:S(2)}, u32[]{:S(2)}) collective-permute-start(bf16[128,512]{1,0:T(8,128)(2,1)S(1)} %slice.18), channel_id=1, source_target_pairs={{0,4},{2,6},{4,0},{6,2},{1,5},{3,7},{5,1},{7,3},{8,12},{10,14},{12... | collective-permute-start | bytes 393224 | tf_op jit(solution)/shard_map/ppermute | solution.py:41
  31.2 3.4 %collective-permute-done.2.refs_3_ = bf16[128,512]{1,0:T(8,128)(2,1)S(1)} collective-permute-done((bf16[128,512]{1,0:T(8,128)(2,1)S(1)}, bf16[128,512]{1,0:T(8,128)(2,1)S(1)}, u32[]{:S(2)}, u32[]{:S(2)}) %collective-permute-start.2) | collective-permute-done | bytes 131104 | tf_op jit(solution)/shard_map/ppermute | solution.py:41
  34.6 1.5 %collective-permute-start.18 = (bf16[128,512]{1,0:T(8,128)(2,1)S(1)}, bf16[128,512]{1,0:T(8,128)(2,1)S(1)}, u32[]{:S(2)}, u32[]{:S(2)}) collective-permute-start(bf16[128,512]{1,0:T(8,128)(2,1)S(1)} %slice.19), channel_id=1, source_target_pairs={{0,2},{2,0},{4,6},{6,4},{1,3},{3,1},{5,7},{7,5},{8,10},{10,8},{12,... | collective-permute-start | bytes 393224 | tf_op jit(solution)/shard_map/ppermute | solution.py:41
  36.1 0.0 collective-permute-done.7.refs_14_
  36.1 2.2 %collective-permute-start.5 = (bf16[128,512]{1,0:T(8,128)(2,1)S(1)}, bf16[128,512]{1,0:T(8,128)(2,1)S(1)}, u32[]{:S(2)}, u32[]{:S(2)}) collective-permute-start(bf16[128,512]{1,0:T(8,128)(2,1)S(1)} %slice.16), channel_id=1, source_target_pairs={{0,4},{2,6},{4,0},{6,2},{1,5},{3,7},{5,1},{7,3},{8,12},{10,14},{12... | collective-permute-start | bytes 393224 | tf_op jit(solution)/shard_map/ppermute | solution.py:41
  38.3 0.0 collective-permute-done.11.refs_1_
  38.3 0.0 collective-permute-start.13
  38.3 0.0 collective-permute-done.20.refs_11_
  38.3 0.5 collective-permute-start.15
  38.8 0.0 collective-permute-done.16.refs_6_
  38.8 0.1 collective-permute-start.21
  38.9 0.7 %collective-permute-done.18.refs_8_ = bf16[128,512]{1,0:T(8,128)(2,1)S(1)} collective-permute-done((bf16[128,512]{1,0:T(8,128)(2,1)S(1)}, bf16[128,512]{1,0:T(8,128)(2,1)S(1)}, u32[]{:S(2)}, u32[]{:S(2)}) %collective-permute-start.18) | collective-permute-done | bytes 131104 | tf_op jit(solution)/shard_map/ppermute | solution.py:41
  39.6 1.5 %collective-permute-start.8 = (bf16[128,512]{1,0:T(8,128)(2,1)S(1)}, bf16[128,512]{1,0:T(8,128)(2,1)S(1)}, u32[]{:S(2)}, u32[]{:S(2)}) collective-permute-start(bf16[128,512]{1,0:T(8,128)(2,1)S(1)} %slice.17), channel_id=1, source_target_pairs={{0,2},{2,0},{4,6},{6,4},{1,3},{3,1},{5,7},{7,5},{8,10},{10,8},{12,... | collective-permute-start | bytes 393224 | tf_op jit(solution)/shard_map/ppermute | solution.py:41
  41.1 0.2 collective-permute-done.5.refs_0_
  41.3 0.0 collective-permute-start.22
  41.3 3.9 %collective-permute-done.8.refs_2_ = bf16[128,512]{1,0:T(8,128)(2,1)S(1)} collective-permute-done((bf16[128,512]{1,0:T(8,128)(2,1)S(1)}, bf16[128,512]{1,0:T(8,128)(2,1)S(1)}, u32[]{:S(2)}, u32[]{:S(2)}) %collective-permute-start.8) | collective-permute-done | bytes 131104 | tf_op jit(solution)/shard_map/ppermute | solution.py:41
  45.3 0.0 collective-permute-start.17
  45.3 0.0 collective-permute-done.13.refs_3_
  45.3 0.5 collective-permute-start.19
  45.8 0.0 collective-permute-done.15.refs_5_
  45.8 0.1 collective-permute-start.6
  45.8 0.0 collective-permute-done.21.refs_13_
  45.8 0.4 collective-permute-start.9
  46.3 1.6 %fetch.1 = (bf16[128,4096]{1,0:T(8,128)(2,1)S(1)}, bf16[128,4096]{1,0:T(8,128)(2,1)S(1)}) custom-call(bf16[128,4096]{1,0:T(8,128)(2,1)} %bitcast.9, bf16[128,4096]{1,0:T(8,128)(2,1)} %bitcast.10), custom_call_target="tpu_custom_call" | custom-call | tf_op jit(solution)/shard_map/fetch/pallas_call | solution.py:108
  47.9 3.0 %attend.1 = (bf16[128,4096]{1,0:T(8,128)(2,1)S(1)}, bf16[128,4096]{1,0:T(8,128)(2,1)S(1)}, f32[128,128]{1,0:T(8,128)S(1)}) custom-call(s32[1,8]{1,0:T(1,128)} %bitcast.15, bf16[128,4096]{1,0:T(8,128)(2,1)S(1)} %get-tuple-element.10.query_ref, bf16[128,4096]{1,0:T(8,128)(2,1)S(1)} %get-tuple-element.11.residual_ref, ...), custom_call_target="tpu_custom_call" | custom-call | tf_op jit(solution)/shard_map/attend/pallas_call | solution.py:202
  50.8 0.0 collective-permute-done.22.refs_15_
  50.8 0.0 collective-permute-done.17.refs_7_
  50.8 0.0 collective-permute-done.19.refs_9_
  50.8 0.7 %project.2.refs_4_ = f32[128,512]{1,0:T(8,128)S(1)} custom-call(bf16[128,4096]{1,0:T(8,128)(2,1)S(1)} %get-tuple-element.14.layer_ref, bf16[256,512]{1,0:T(8,128)(2,1)S(1)} %collective-permute-done.10.refs_0_, bf16[256,512]{1,0:T(8,128)(2,1)S(1)} %collective-permute-done.11.refs_1_, bf16[256,512]{1,0:T(8,128)(2,1)S(1)} %collective-permute-done.12.refs_2_, ...), custom_call_target="tpu_custom_call" | custom-call | tf_op jit(solution)/shard_map/project/pallas_call | solution.py:246
  51.6 0.0 collective-permute-done.6.refs_1_
  51.6 0.0 collective-permute-done.9.refs_3_
  51.6 0.3 project.3
  51.9 3.5 %collective-permute-start.23 = (bf16[128,512]{1,0:T(8,128)(2,1)S(1)}, bf16[128,512]{1,0:T(8,128)(2,1)S(1)}, u32[]{:S(2)}, u32[]{:S(2)}) collective-permute-start(bf16[128,512]{1,0:T(8,128)(2,1)S(1)} %project.3), channel_id=1, source_target_pairs={{0,8},{8,16},{16,24},{1,9},{9,17},{17,25},{2,10},{10,18},{18,26},{... | collective-permute-start | bytes 393224 | tf_op jit(solution)/shard_map/ppermute | solution.py:37
  55.4 1.0 %copy.10 = bf16[1,1,128,4096]{3,2,1,0:T(8,128)(2,1)} copy(bf16[1,1,128,4096]{3,2,1,0:T(8,128)(2,1)S(1)} %bitcast.8) | data formatting | bytes 2097152
  56.3 2.0 %collective-permute-done.23 = bf16[128,512]{1,0:T(8,128)(2,1)S(1)} collective-permute-done((bf16[128,512]{1,0:T(8,128)(2,1)S(1)}, bf16[128,512]{1,0:T(8,128)(2,1)S(1)}, u32[]{:S(2)}, u32[]{:S(2)}) %collective-permute-start.23) | collective-permute-done | bytes 131104 | tf_op jit(solution)/shard_map/ppermute | solution.py:37
  58.3 0.7 %copy.11 = bf16[1,1,128,512]{3,2,1,0:T(8,128)(2,1)} copy(bf16[1,1,128,512]{3,2,1,0:T(8,128)(2,1)S(1)} %bitcast.12) | data formatting | bytes 262144
  (4 shorter events, 0.0 us)
Async XLA Ops:
  1.9 12.1 %collective-permute-start.10 = (bf16[256,512]{1,0:T(8,128)(2,1)S(1)}, bf16[256,512]{1,0:T(8,128)(2,1)S(1)}, u32[]{:S(2)}, u32[]{:S(2)}) collective-permute-start(bf16[256,512]{1,0:T(8,128)(2,1)S(1)} %get-tuple-element.16), channel_id=1, source_target_pairs={{8,0},{16,8},{24,16},{9,1},{17,9},{25,17},{10,2},{18,10},{26,18},{... | collective-permute-start | bytes 786440 | tf_op jit(solution)/shard_map/ppermute | solution.py:37
  3.2 15.6 %collective-permute-start.3 = (bf16[256,512]{1,0:T(8,128)(2,1)S(1)}, bf16[256,512]{1,0:T(8,128)(2,1)S(1)}, u32[]{:S(2)}, u32[]{:S(2)}) collective-permute-start(bf16[256,512]{1,0:T(8,128)(2,1)S(1)} %get-tuple-element.15), channel_id=1, source_target_pairs={{8,0},{16,8},{24,16},{9,1},{17,9},{25,17},{10,2},{18,10},{26,18},{... | collective-permute-start | bytes 786440 | tf_op jit(solution)/shard_map/ppermute | solution.py:37
  14.0 13.6 %collective-permute-start.12 = (bf16[256,512]{1,0:T(8,128)(2,1)S(1)}, bf16[256,512]{1,0:T(8,128)(2,1)S(1)}, u32[]{:S(2)}, u32[]{:S(2)}) collective-permute-start(bf16[256,512]{1,0:T(8,128)(2,1)S(1)} %collective-permute-done.10.refs_0_), channel_id=1, source_target_pairs={{0,2},{2,0},{4,6},{6,4},{1,3},{3,1},{5,7},{7,5},{8,10},{10,8},{12,... | collective-permute-start | bytes 786440 | tf_op jit(solution)/shard_map/ppermute | solution.py:41
  15.9 12.2 %collective-permute-start.14 = (bf16[256,512]{1,0:T(8,128)(2,1)S(1)}, bf16[256,512]{1,0:T(8,128)(2,1)S(1)}, u32[]{:S(2)}, u32[]{:S(2)}) collective-permute-start(bf16[256,512]{1,0:T(8,128)(2,1)S(1)} %collective-permute-done.10.refs_0_), channel_id=1, source_target_pairs={{0,4},{2,6},{4,0},{6,2},{1,5},{3,7},{5,1},{7,3},{8,12},{10,14},{12... | collective-permute-start | bytes 786440 | tf_op jit(solution)/shard_map/ppermute | solution.py:41
  17.4 8.5 %collective-permute-start = (bf16[128,512]{1,0:T(8,128)(2,1)S(1)}, bf16[128,512]{1,0:T(8,128)(2,1)S(1)}, u32[]{:S(2)}, u32[]{:S(2)}) collective-permute-start(bf16[128,512]{1,0:T(8,128)(2,1)S(1)} %get-tuple-element.12.refs_0_), channel_id=1, source_target_pairs={{0,2},{2,0},{4,6},{6,4},{1,3},{3,1},{5,7},{7,5},{8,10},{10,8},{12,... | collective-permute-start | bytes 393224 | tf_op jit(solution)/shard_map/ppermute | solution.py:41
  18.0 9.6 %collective-permute-start.1 = (bf16[128,512]{1,0:T(8,128)(2,1)S(1)}, bf16[128,512]{1,0:T(8,128)(2,1)S(1)}, u32[]{:S(2)}, u32[]{:S(2)}) collective-permute-start(bf16[128,512]{1,0:T(8,128)(2,1)S(1)} %get-tuple-element.12.refs_0_), channel_id=1, source_target_pairs={{0,4},{2,6},{4,0},{6,2},{1,5},{3,7},{5,1},{7,3},{8,12},{10,14},{12... | collective-permute-start | bytes 393224 | tf_op jit(solution)/shard_map/ppermute | solution.py:41
  18.8 10.8 %collective-permute-start.4 = (bf16[256,512]{1,0:T(8,128)(2,1)S(1)}, bf16[256,512]{1,0:T(8,128)(2,1)S(1)}, u32[]{:S(2)}, u32[]{:S(2)}) collective-permute-start(bf16[256,512]{1,0:T(8,128)(2,1)S(1)} %collective-permute-done.3.refs_10_), channel_id=1, source_target_pairs={{0,2},{2,0},{4,6},{6,4},{1,3},{3,1},{5,7},{7,5},{8,10},{10,8},{12,... | collective-permute-start | bytes 786440 | tf_op jit(solution)/shard_map/ppermute | solution.py:41
  26.0 10.1 %collective-permute-start.7 = (bf16[256,512]{1,0:T(8,128)(2,1)S(1)}, bf16[256,512]{1,0:T(8,128)(2,1)S(1)}, u32[]{:S(2)}, u32[]{:S(2)}) collective-permute-start(bf16[256,512]{1,0:T(8,128)(2,1)S(1)} %collective-permute-done.3.refs_10_), channel_id=1, source_target_pairs={{0,4},{2,6},{4,0},{6,2},{1,5},{3,7},{5,1},{7,3},{8,12},{10,14},{12... | collective-permute-start | bytes 786440 | tf_op jit(solution)/shard_map/ppermute | solution.py:41
  27.6 10.7 %collective-permute-start.11 = (bf16[256,512]{1,0:T(8,128)(2,1)S(1)}, bf16[256,512]{1,0:T(8,128)(2,1)S(1)}, u32[]{:S(2)}, u32[]{:S(2)}) collective-permute-start(bf16[256,512]{1,0:T(8,128)(2,1)S(1)} %collective-permute-done.10.refs_0_), channel_id=1, source_target_pairs={{0,1},{1,0},{2,3},{3,2},{4,5},{5,4},{6,7},{7,6},{8,9},{9,8},{10,11... | collective-permute-start | bytes 786440 | tf_op jit(solution)/shard_map/ppermute | solution.py:41
  27.6 10.7 %collective-permute-start.20 = (bf16[256,512]{1,0:T(8,128)(2,1)S(1)}, bf16[256,512]{1,0:T(8,128)(2,1)S(1)}, u32[]{:S(2)}, u32[]{:S(2)}) collective-permute-start(bf16[256,512]{1,0:T(8,128)(2,1)S(1)} %collective-permute-done.3.refs_10_), channel_id=1, source_target_pairs={{0,1},{1,0},{2,3},{3,2},{4,5},{5,4},{6,7},{7,6},{8,9},{9,8},{10,11... | collective-permute-start | bytes 786440 | tf_op jit(solution)/shard_map/ppermute | solution.py:41
  28.1 6.5 %collective-permute-start.2 = (bf16[128,512]{1,0:T(8,128)(2,1)S(1)}, bf16[128,512]{1,0:T(8,128)(2,1)S(1)}, u32[]{:S(2)}, u32[]{:S(2)}) collective-permute-start(bf16[128,512]{1,0:T(8,128)(2,1)S(1)} %get-tuple-element.12.refs_0_), channel_id=1, source_target_pairs={{0,6},{2,4},{4,2},{6,0},{1,7},{3,5},{5,3},{7,1},{8,14},{10,12},{12... | collective-permute-start | bytes 393224 | tf_op jit(solution)/shard_map/ppermute | solution.py:41
  29.6 9.2 %collective-permute-start.16 = (bf16[128,512]{1,0:T(8,128)(2,1)S(1)}, bf16[128,512]{1,0:T(8,128)(2,1)S(1)}, u32[]{:S(2)}, u32[]{:S(2)}) collective-permute-start(bf16[128,512]{1,0:T(8,128)(2,1)S(1)} %slice.18), channel_id=1, source_target_pairs={{0,4},{2,6},{4,0},{6,2},{1,5},{3,7},{5,1},{7,3},{8,12},{10,14},{12... | collective-permute-start | bytes 393224 | tf_op jit(solution)/shard_map/ppermute | solution.py:41
  34.6 5.0 %collective-permute-start.18 = (bf16[128,512]{1,0:T(8,128)(2,1)S(1)}, bf16[128,512]{1,0:T(8,128)(2,1)S(1)}, u32[]{:S(2)}, u32[]{:S(2)}) collective-permute-start(bf16[128,512]{1,0:T(8,128)(2,1)S(1)} %slice.19), channel_id=1, source_target_pairs={{0,2},{2,0},{4,6},{6,4},{1,3},{3,1},{5,7},{7,5},{8,10},{10,8},{12,... | collective-permute-start | bytes 393224 | tf_op jit(solution)/shard_map/ppermute | solution.py:41
  36.1 5.2 %collective-permute-start.5 = (bf16[128,512]{1,0:T(8,128)(2,1)S(1)}, bf16[128,512]{1,0:T(8,128)(2,1)S(1)}, u32[]{:S(2)}, u32[]{:S(2)}) collective-permute-start(bf16[128,512]{1,0:T(8,128)(2,1)S(1)} %slice.16), channel_id=1, source_target_pairs={{0,4},{2,6},{4,0},{6,2},{1,5},{3,7},{5,1},{7,3},{8,12},{10,14},{12... | collective-permute-start | bytes 393224 | tf_op jit(solution)/shard_map/ppermute | solution.py:41
  38.3 6.9 %collective-permute-start.13 = (bf16[256,512]{1,0:T(8,128)(2,1)S(1)}, bf16[256,512]{1,0:T(8,128)(2,1)S(1)}, u32[]{:S(2)}, u32[]{:S(2)}) collective-permute-start(bf16[256,512]{1,0:T(8,128)(2,1)S(1)} %collective-permute-done.12.refs_2_), channel_id=1, source_target_pairs={{0,1},{1,0},{2,3},{3,2},{4,5},{5,4},{6,7},{7,6},{8,9},{9,8},{10,11... | collective-permute-start | bytes 786440 | tf_op jit(solution)/shard_map/ppermute | solution.py:41
  38.3 7.4 %collective-permute-start.15 = (bf16[256,512]{1,0:T(8,128)(2,1)S(1)}, bf16[256,512]{1,0:T(8,128)(2,1)S(1)}, u32[]{:S(2)}, u32[]{:S(2)}) collective-permute-start(bf16[256,512]{1,0:T(8,128)(2,1)S(1)} %collective-permute-done.14.refs_4_), channel_id=1, source_target_pairs={{0,1},{1,0},{2,3},{3,2},{4,5},{5,4},{6,7},{7,6},{8,9},{9,8},{10,11... | collective-permute-start | bytes 786440 | tf_op jit(solution)/shard_map/ppermute | solution.py:41
  38.8 7.0 %collective-permute-start.21 = (bf16[256,512]{1,0:T(8,128)(2,1)S(1)}, bf16[256,512]{1,0:T(8,128)(2,1)S(1)}, u32[]{:S(2)}, u32[]{:S(2)}) collective-permute-start(bf16[256,512]{1,0:T(8,128)(2,1)S(1)} %collective-permute-done.4.refs_12_), channel_id=1, source_target_pairs={{0,1},{1,0},{2,3},{3,2},{4,5},{5,4},{6,7},{7,6},{8,9},{9,8},{10,11... | collective-permute-start | bytes 786440 | tf_op jit(solution)/shard_map/ppermute | solution.py:41
  39.6 5.7 %collective-permute-start.8 = (bf16[128,512]{1,0:T(8,128)(2,1)S(1)}, bf16[128,512]{1,0:T(8,128)(2,1)S(1)}, u32[]{:S(2)}, u32[]{:S(2)}) collective-permute-start(bf16[128,512]{1,0:T(8,128)(2,1)S(1)} %slice.17), channel_id=1, source_target_pairs={{0,2},{2,0},{4,6},{6,4},{1,3},{3,1},{5,7},{7,5},{8,10},{10,8},{12,... | collective-permute-start | bytes 393224 | tf_op jit(solution)/shard_map/ppermute | solution.py:41
  41.3 9.5 %collective-permute-start.22 = (bf16[256,512]{1,0:T(8,128)(2,1)S(1)}, bf16[256,512]{1,0:T(8,128)(2,1)S(1)}, u32[]{:S(2)}, u32[]{:S(2)}) collective-permute-start(bf16[256,512]{1,0:T(8,128)(2,1)S(1)} %collective-permute-done.7.refs_14_), channel_id=1, source_target_pairs={{0,1},{1,0},{2,3},{3,2},{4,5},{5,4},{6,7},{7,6},{8,9},{9,8},{10,11... | collective-permute-start | bytes 786440 | tf_op jit(solution)/shard_map/ppermute | solution.py:41
  45.3 5.6 %collective-permute-start.17 = (bf16[128,512]{1,0:T(8,128)(2,1)S(1)}, bf16[128,512]{1,0:T(8,128)(2,1)S(1)}, u32[]{:S(2)}, u32[]{:S(2)}) collective-permute-start(bf16[128,512]{1,0:T(8,128)(2,1)S(1)} %collective-permute-done.16.refs_6_), channel_id=1, source_target_pairs={{0,1},{1,0},{2,3},{3,2},{4,5},{5,4},{6,7},{7,6},{8,9},{9,8},{10,11... | collective-permute-start | bytes 393224 | tf_op jit(solution)/shard_map/ppermute | solution.py:41
  45.3 5.6 %collective-permute-start.19 = (bf16[128,512]{1,0:T(8,128)(2,1)S(1)}, bf16[128,512]{1,0:T(8,128)(2,1)S(1)}, u32[]{:S(2)}, u32[]{:S(2)}) collective-permute-start(bf16[128,512]{1,0:T(8,128)(2,1)S(1)} %collective-permute-done.18.refs_8_), channel_id=1, source_target_pairs={{0,1},{1,0},{2,3},{3,2},{4,5},{5,4},{6,7},{7,6},{8,9},{9,8},{10,11... | collective-permute-start | bytes 393224 | tf_op jit(solution)/shard_map/ppermute | solution.py:41
  45.8 5.8 %collective-permute-start.6 = (bf16[128,512]{1,0:T(8,128)(2,1)S(1)}, bf16[128,512]{1,0:T(8,128)(2,1)S(1)}, u32[]{:S(2)}, u32[]{:S(2)}) collective-permute-start(bf16[128,512]{1,0:T(8,128)(2,1)S(1)} %collective-permute-done.5.refs_0_), channel_id=1, source_target_pairs={{0,1},{1,0},{2,3},{3,2},{4,5},{5,4},{6,7},{7,6},{8,9},{9,8},{10,11... | collective-permute-start | bytes 393224 | tf_op jit(solution)/shard_map/ppermute | solution.py:41
  45.8 5.8 %collective-permute-start.9 = (bf16[128,512]{1,0:T(8,128)(2,1)S(1)}, bf16[128,512]{1,0:T(8,128)(2,1)S(1)}, u32[]{:S(2)}, u32[]{:S(2)}) collective-permute-start(bf16[128,512]{1,0:T(8,128)(2,1)S(1)} %collective-permute-done.8.refs_2_), channel_id=1, source_target_pairs={{0,1},{1,0},{2,3},{3,2},{4,5},{5,4},{6,7},{7,6},{8,9},{9,8},{10,11... | collective-permute-start | bytes 393224 | tf_op jit(solution)/shard_map/ppermute | solution.py:41
  51.9 6.4 %collective-permute-start.23 = (bf16[128,512]{1,0:T(8,128)(2,1)S(1)}, bf16[128,512]{1,0:T(8,128)(2,1)S(1)}, u32[]{:S(2)}, u32[]{:S(2)}) collective-permute-start(bf16[128,512]{1,0:T(8,128)(2,1)S(1)} %project.3), channel_id=1, source_target_pairs={{0,8},{8,16},{16,24},{1,9},{9,17},{17,25},{2,10},{10,18},{18,26},{... | collective-permute-start | bytes 393224 | tf_op jit(solution)/shard_map/ppermute | solution.py:37
where the time goes:
time: 59.2 us; the launch traced here: 59 us
  waiting for transfers between devices  26 us (44%)
  starting transfers between devices  23.8 us (40%)
  Pallas kernels  6.79 us (11%)
  local copies, waits for them, and re-layouts  1.67 us (3%)
  between operations  0.78 us (1%)
    ppermute x21, starting transfers between devices, exchanged(): lax.ppermute(block, axis, [(i, i ^ bit) for i in range(lax.axis_size(axis...  17.7 us
    ppermute x21, waiting for transfers between devices, exchanged(): lax.ppermute(block, axis, [(i, i ^ bit) for i in range(lax.axis_size(axis...  13.8 us
    ppermute x3, waiting for transfers between devices, shifted(): return lax.ppermute(block, 'pipe', route)  12.2 us
    ppermute x3, starting transfers between devices, shifted(): return lax.ppermute(block, 'pipe', route)  6.04 us
    pallas_call x1, Pallas kernels, attend(): pl.pallas_call(functools.partial(attend_kernel, groups, longest, 1.0 / ma...  2.96 us
    unnamed x2, local copies, waits for them, and re-layouts  1.63 us
    pallas_call x1, Pallas kernels, fetch(): pl.pallas_call(fetch_kernel, out_shape=tuple((pltpu.VMEM(array.shape, arr...  1.56 us
    pallas_call x1, Pallas kernels, prepare(): pl.pallas_call(prepare_kernel, out_shape=(pltpu.VMEM((rows, 2 * width), k...  1.25 us
  transfers between devices with their start and end apart: 24, of which 8 were waited for; matrix products, arithmetic and copies ran while one was open for 2% of the time, Pallas kernels for 9%

commit v1 on v0

--- a/solution.py
+++ b/solution.py
@@ -48,8 +48,14 @@
         copy.wait()
 
 
-def prepare_kernel(key_ref, value_ref, gain_ref, weight_ref, pair_ref, *refs):
+def sent_half(device, groups):
+    return (device >= groups // 2).astype(jnp.int32)
+
+
+def prepare_kernel(key_ref, value_ref, gain_ref, weight_ref, pair_ref, half_ref, *refs):
     piece_refs, (weight, gain, sems) = refs[:-3], refs[-3:]
+    half = half_ref.shape[0]
+    sent = pl.ds(pl.multiple_of(sent_half(lax.axis_index("seq"), lax.axis_size("seq")) * half, half), half)
     width = key_ref.shape[1]
     depth = weight_ref.shape[0]
     at = (lax.axis_index("seq") * lax.axis_size("exp") + lax.axis_index("exp")) * depth
@@ -59,6 +65,8 @@
             pltpu.make_async_copy(gain_ref, gain, sems.at[1]),
             pltpu.make_async_copy(key_ref, pair_ref.at[:, :width], sems.at[2]),
             pltpu.make_async_copy(value_ref, pair_ref.at[:, width:], sems.at[3]),
+            pltpu.make_async_copy(key_ref.at[sent], half_ref.at[:, :width], sems.at[4]),
+            pltpu.make_async_copy(value_ref.at[sent], half_ref.at[:, width:], sems.at[5]),
         ]
     )
     if depth % DH:
@@ -83,13 +91,17 @@
     piece = pltpu.VMEM((depth // pieces, cols), weight.dtype)
     return pl.pallas_call(
         prepare_kernel,
-        out_shape=(pltpu.VMEM((rows, 2 * width), key_rows.dtype), *[piece] * pieces),
+        out_shape=(
+            pltpu.VMEM((rows, 2 * width), key_rows.dtype),
+            pltpu.VMEM((rows // 2, 2 * width), key_rows.dtype),
+            *[piece] * pieces,
+        ),
         in_specs=[FAR] * 4,
-        out_specs=(WHOLE,) * (1 + pieces),
+        out_specs=(WHOLE,) * (2 + pieces),
         scratch_shapes=[
             pltpu.VMEM((depth, cols), weight.dtype),
             pltpu.VMEM(norm_gain.shape, jnp.float32),
-            pltpu.SemaphoreType.DMA((4,)),
+            pltpu.SemaphoreType.DMA((6,)),
         ],
         compiler_params=budget(6),
         name="prepare",
@@ -116,8 +128,25 @@
     )(*[far(array) for array in arrays])
 
 
-def attend_kernel(groups, longest, score_scale, far_lengths_ref, query_ref, residual_ref, *refs):
-    pair_refs, (context_ref, layer_ref, inverse_ref, every, lengths_ref, sem) = refs[:-6], refs[-6:]
+def store_kernel(near_ref, far_ref, sem):
+    run_copies([pltpu.make_async_copy(near_ref, far_ref, sem)])
+
+
+def store(array):
+    return pl.pallas_call(
+        store_kernel,
+        out_shape=jax.ShapeDtypeStruct(array.shape, array.dtype),
+        in_specs=[WHOLE],
+        out_specs=FAR,
+        scratch_shapes=[pltpu.SemaphoreType.DMA],
+        compiler_params=budget(2),
+        name="store",
+    )(near(array))
+
+
+def attend_kernel(groups, longest, score_scale, stays, far_lengths_ref, query_ref, residual_ref, *refs):
+    pair_refs, outs = refs[: -len(stays) - 5], refs[-len(stays) - 5 :]
+    context_ref, inverse_ref, *layer_refs, every, lengths_ref, sem = outs
     lengths_copy = pltpu.make_async_copy(far_lengths_ref, lengths_ref, sem)
     lengths_copy.start()
     tok_rows, row_width = query_ref.shape
@@ -132,7 +161,12 @@
         every[...] = pair_refs[0][...].reshape(every.shape)
     else:
         for bit, pair_ref in enumerate(pair_refs):
-            every[own ^ bit] = pair_ref[...]
+            sender, rows = own ^ bit, pair_ref.shape[0]
+            if rows == tok_rows:
+                every[sender] = pair_ref[...]
+            else:
+                at = pl.multiple_of(sent_half(sender, groups) * rows, rows)
+                every[sender, pl.ds(at, rows), :] = pair_ref[...]
     lengths_copy.wait()
     bounds = []
     total = jnp.int32(0)
@@ -140,6 +174,12 @@
         total = total + lengths_ref[0, doc]
         bounds.append(total)
     exponent = score_scale * math.log2(math.e)
+    places = {head: (ref, at) for ref, heads in zip(layer_refs, stays) for at, head in enumerate(heads)}
+
+    def put(rows, head, block):
+        ref, at = places[head]
+        ref[rows, at * DH : (at + 1) * DH] = block
+
     for run in range(2):
         block = own if run == 0 else 2 * groups - 1 - own
         first_pos = block * half_rows
@@ -187,23 +227,32 @@
                 added = (
                     residual_ref[rows, cols].astype(jnp.float32) + context[h].astype(jnp.float32)
                 ).astype(jnp.bfloat16)
-                layer_ref[rows, cols] = added
+                put(rows, group * per_kv + h, added)
                 wide = added.astype(jnp.float32)
                 squares = squares + wide * wide
         mean_square = jnp.sum(squares, axis=1, keepdims=True) * (1.0 / row_width)
-        inverse_ref[rows, :] = jnp.broadcast_to(lax.rsqrt(mean_square + epsilon), (half_rows, DH))
-
-
-def attend(lengths, queries, residual, pairs, groups):
+        inverse = lax.rsqrt(mean_square + epsilon)
+        inverse_ref[rows, :] = jnp.broadcast_to(inverse, (half_rows, DH))
+        for ref in layer_refs[1:]:
+            for left in range(0, ref.shape[1], DH):
+                cols = slice(left, left + DH)
+                ref[rows, cols] = (ref[rows, cols].astype(jnp.float32) * inverse).astype(jnp.bfloat16)
+
+
+def attend(lengths, queries, residual, pairs, groups, stays):
     tok_rows, _ = queries.shape
     longest = tok_rows * groups // 4
     pair_width = pairs[0].shape[1]
     shape = pltpu.VMEM(queries.shape, jnp.bfloat16)
     return pl.pallas_call(
-        functools.partial(attend_kernel, groups, longest, 1.0 / math.sqrt(DH)),
-        out_shape=(shape, shape, pltpu.VMEM((tok_rows, DH), jnp.float32)),
+        functools.partial(attend_kernel, groups, longest, 1.0 / math.sqrt(DH), stays),
+        out_shape=(
+            shape,
+            pltpu.VMEM((tok_rows, DH), jnp.float32),
+            *[pltpu.VMEM((tok_rows, DH * len(heads)), jnp.bfloat16) for heads in stays],
+        ),
         in_specs=[FAR] + [WHOLE] * (2 + len(pairs)),
-        out_specs=(WHOLE,) * 3,
+        out_specs=(WHOLE,) * (2 + len(stays)),
         scratch_shapes=[
             pltpu.VMEM((groups, tok_rows, pair_width), jnp.bfloat16),
             pltpu.SMEM(lengths.shape, jnp.int32),
@@ -214,13 +263,12 @@
     )(far(lengths), *[near(array) for array in (queries, residual, *pairs)])
 
 
-def project_kernel(places, last, layer_ref, *refs):
+def project_kernel(places, scaled, layer_ref, *refs):
     piece_refs = refs[: len(places)]
-    rest = refs[len(places) :]
-    out_ref = rest[-1]
+    *rest, out_ref = refs[len(places) :]
     depth = layer_ref.shape[1] // (lax.axis_size("seq") * lax.axis_size("exp"))
     seq, core = lax.axis_index("seq"), lax.axis_index("exp")
-    total = None if len(rest) == 1 else rest[0][...]
+    total = rest[0][...] if len(rest) > scaled else None
     for (bit, kind, first), piece_ref in zip(places, piece_refs):
         rows = piece_ref.shape[0]
         column = ((seq ^ bit) * 2 + (core ^ kind)) * depth + first
@@ -228,24 +276,23 @@
             layer_ref[:, pl.ds(pl.multiple_of(column, DH), rows)], piece_ref[...], preferred_element_type=jnp.float32
         )
         total = part if total is None else total + part
-    if last:
-        inverse_ref = rest[1]
+    if scaled:
         for left in range(0, total.shape[1], DH):
             cols = slice(left, left + DH)
-            out_ref[:, cols] = (total[:, cols] * inverse_ref[...]).astype(jnp.bfloat16)
+            out_ref[:, cols] = (total[:, cols] * rest[-1][...]).astype(jnp.bfloat16)
     else:
         out_ref[...] = total
 
 
 def project(layer, held, so_far=None, inverse=None):
     places = tuple(held)
-    last = inverse is not None
+    scaled = inverse is not None
     blocks = [held[place] for place in places]
     extra = [array for array in (so_far, inverse) if array is not None]
     shape = (layer.shape[0], blocks[0].shape[1])
     return pl.pallas_call(
-        functools.partial(project_kernel, places, last),
-        out_shape=pltpu.VMEM(shape, jnp.bfloat16 if last else jnp.float32),
+        functools.partial(project_kernel, places, scaled),
+        out_shape=pltpu.VMEM(shape, jnp.bfloat16 if scaled else jnp.float32),
         in_specs=[WHOLE] * (1 + len(blocks) + len(extra)),
         out_specs=WHOLE,
         compiler_params=budget(8),
@@ -253,42 +300,55 @@
     )(*[near(array) for array in (layer, *blocks, *extra)])
 
 
+def gather_square(block, relays):
+    early, late = {}, {}
+
+    def hold(held, bit, first, piece):
+        held[bit, 0, first] = piece
+        held[bit, 1, first] = exchanged(piece, "exp", 1)
+
+    hold(early, 0, 0, block)
+    sides = {}
+    for bit in (1, 2):
+        sides[bit] = exchanged(block, "seq", bit)
+        hold(early, bit, 0, sides[bit])
+    part = block.shape[0] // len(relays)
+    for index, bit in enumerate(relays):
+        start = index * part
+        corner = exchanged(sides[bit][start : start + part], "seq", 3 - bit)
+        hold(late, 3, start, corner)
+    return early, late
+
+
 def square_of_chips(queries, key_rows, value_rows, residual, lengths, norm_gain, weight):
-    pair, *parts = prepare(key_rows, value_rows, norm_gain, weight, 2)
-    early, late = {}, {}
-
-    def hold(held, bit, first, block):
-        held[bit, 0, first] = block
-        held[bit, 1, first] = exchanged(block, "exp", 1)
-
-    first = 0
-    for index, part in enumerate(parts):
-        block = shifted(part, -1)
-        hold(early, 0, first, block)
-        sides = {}
-        for bit in (1, 2):
-            sides[bit] = exchanged(block, "seq", bit)
-            hold(early, bit, first, sides[bit])
-        half = block.shape[0] // 2
-        for bit in (1, 2):
-            start = (bit - 1) * half
-            corner = exchanged(sides[bit][start : start + half], "seq", 3 - bit)
-            hold(early if index == 0 else late, 3, first + start, corner)
-        first += block.shape[0]
-    pairs = [pair]
-    for bit in (1, 2, 3):
-        pairs.append(exchanged(pair, "seq", bit))
+    pair, half, leaves, stays = prepare(key_rows, value_rows, norm_gain, weight, 2)
+    leaves = shifted(leaves, -1)
+    leaves_early, leaves_late = gather_square(leaves, (1, 2))
+    stays_early, stays_late = gather_square(stays, (2,))
+    pairs = [pair, exchanged(pair, "seq", 1)]
+    pairs.append(exchanged(half, "seq", 2))
+    pairs.append(exchanged(half, "seq", 3))
     queries, residual = fetch(queries, residual)
-    context, layer, inverse = attend(lengths, queries, residual, pairs, lax.axis_size("seq"))
-    so_far = project(layer, early)
-    projected = project(layer, late, so_far, inverse)
-    return context, shifted(projected, 1)
+    per_block = weight.shape[0] // DH
+    heads = range(queries.shape[1] // DH)
+    parts = [[head for head in heads if (head % per_block < per_block // 2) == first] for first in (True, False)]
+    context, inverse, layer, normed = attend(
+        lengths, queries, residual, pairs, lax.axis_size("seq"), parts
+    )
+    context = store(context)
+    received = shifted(normed, 1)
+    so_far = project(layer, leaves_early)
+    projected = project(layer, leaves_late, so_far, inverse)
+    arrived = shifted(projected, 1)
+    total = project(received, {**stays_early, **stays_late})
+    return context, (arrived.astype(jnp.float32) + total).astype(jnp.bfloat16)
 
 
 def any_mesh(queries, key_rows, value_rows, residual, lengths, norm_gain, weight):
-    pair, part = prepare(key_rows, value_rows, norm_gain, weight, 1)
+    pair, _, part = prepare(key_rows, value_rows, norm_gain, weight, 1)
     pairs = [lax.all_gather(pair, "seq", axis=0, tiled=True)]
-    context, layer, inverse = attend(lengths, queries, residual, pairs, lax.axis_size("seq"))
+    heads = [list(range(queries.shape[1] // DH))]
+    context, inverse, layer = attend(lengths, queries, residual, pairs, lax.axis_size("seq"), heads)
     every = lax.all_gather(shifted(part, -1), ("seq", "exp"), axis=0, tiled=True)
     total = jnp.dot(layer, every, preferred_element_type=jnp.float32)
     return context, shifted((total * inverse[:, :1]).astype(jnp.bfloat16), 1)

time: 59.2 us -> 52.3 us (0.88)
  waiting for transfers between devices: 26 us -> 17.6 us
  local copies, waits for them, and re-layouts: 1.67 us -> 0.02 us
  starting transfers between devices: 23.8 us -> 25.1 us
  Pallas kernels: 6.79 us -> 7.99 us
  other arithmetic: 0 us -> 0.68 us
    ppermute x21 -> x19, waiting for transfers between devices: 13.8 us -> 6.85 us  [exchanged(): lax.ppermute(block, axis, [(i, i ^ bit) for i in range(lax.axis_size(axis...]
    ppermute x3, starting transfers between devices: 6.04 us -> 8.27 us  [shifted(): return lax.ppermute(block, 'pipe', route)]
    unnamed x2 -> x0, local copies, waits for them, and re-layouts: 1.63 us -> none
    ppermute x3, waiting for transfers between devices: 12.2 us -> 10.7 us  [shifted(): return lax.ppermute(block, 'pipe', route)]
    pallas_call x2 -> x4, Pallas kernels: 1.03 us -> 2.12 us  [the longest x3 1.14 us: project(): pl.pallas_call(functools.partial(project_kernel, places, scaled), out_sha...]
    ppermute x21 -> x19, starting transfers between devices: 17.7 us -> 16.8 us  [exchanged(): lax.ppermute(block, axis, [(i, i ^ bit) for i in range(lax.axis_size(axis...]
    broadcast_in_dim x0 -> x1, other arithmetic: none -> 0.68 us  [on_device(): return (context[None, None], kv_next[None, None])]
  transfers between devices with their start and end apart: 24 -> 22, of which waited for: 8 -> 8; matrix products, arithmetic and copies ran while one was open for 2% -> 0% of each run, Pallas kernels for 9% -> 13%
where the time goes in v1:
time: 52.3 us; the launch traced here: 52.1 us
  starting transfers between devices  25.1 us (48%)
  waiting for transfers between devices  17.6 us (34%)
  Pallas kernels  7.99 us (15%)
  between operations  0.8 us (2%)
  other arithmetic  0.68 us (1%)
    ppermute x19, starting transfers between devices, exchanged(): lax.ppermute(block, axis, [(i, i ^ bit) for i in range(lax.axis_size(axis...  16.8 us
    ppermute x3, waiting for transfers between devices, shifted(): return lax.ppermute(block, 'pipe', route)  10.7 us
    ppermute x3, starting transfers between devices, shifted(): return lax.ppermute(block, 'pipe', route)  8.27 us
    ppermute x19, waiting for transfers between devices, exchanged(): lax.ppermute(block, axis, [(i, i ^ bit) for i in range(lax.axis_size(axis...  6.85 us
    pallas_call x1, Pallas kernels, attend(): pl.pallas_call(functools.partial(attend_kernel, groups, longest, 1.0 / ma...  3.04 us
    pallas_call x1, Pallas kernels, fetch(): pl.pallas_call(fetch_kernel, out_shape=tuple((pltpu.VMEM(array.shape, arr...  1.56 us
    pallas_call x1, Pallas kernels, prepare(): pl.pallas_call(prepare_kernel, out_shape=(pltpu.VMEM((rows, 2 * width), k...  1.27 us
    pallas_call x3, Pallas kernels, project(): pl.pallas_call(functools.partial(project_kernel, places, scaled), out_sha...  1.14 us
  transfers between devices with their start and end apart: 22, of which 8 were waited for; matrix products, arithmetic and copies ran while one was open for 0% of the time, Pallas kernels for 13%

profile of v1, /device:TPU:0, one launch (start us, length us, event | category | flops | bytes accessed | tf_op | source)
XLA Modules:
  0.0 52.1 jit_solution(10700743051432002412)
XLA Ops:
  0.6 1.3 %prepare.1 = (bf16[128,512]{1,0:T(8,128)(2,1)S(1)}, bf16[64,512]{1,0:T(8,128)(2,1)S(1)}, bf16[256,512]{1,0:T(8,128)(2,1)S(1)}, bf16[256,512]{1,0:T(8,128)(2,1)S(1)}) custom-call(bf16[128,256]{1,0:T(8,128)(2,1)} %bitcast.13, bf16[128,256]{1,0:T(8,128)(2,1)} %bitcast.14, f32[1,4096]{1,0:T(1,128)} %gain_ref.1, bf16[512,512]{1,0:T(8,128)(2,1)} %bitcast.12), custom_call_target="tpu_custom_call" | custom-call | tf_op jit(solution)/shard_map/prepare/pallas_call | solution.py:92
  1.9 1.3 %collective-permute-start.3 = (bf16[256,512]{1,0:T(8,128)(2,1)S(1)}, bf16[256,512]{1,0:T(8,128)(2,1)S(1)}, u32[]{:S(2)}, u32[]{:S(2)}) collective-permute-start(bf16[256,512]{1,0:T(8,128)(2,1)S(1)} %get-tuple-element.18), channel_id=1, source_target_pairs={{8,0},{16,8},{24,16},{9,1},{17,9},{25,17},{10,2},{18,10},{26,18},{... | collective-permute-start | bytes 786440 | tf_op jit(solution)/shard_map/ppermute | solution.py:37
  3.2 3.1 %collective-permute-start.18 = (bf16[256,512]{1,0:T(8,128)(2,1)S(1)}, bf16[256,512]{1,0:T(8,128)(2,1)S(1)}, u32[]{:S(2)}, u32[]{:S(2)}) collective-permute-start(bf16[256,512]{1,0:T(8,128)(2,1)S(1)} %get-tuple-element.21.refs_0_), channel_id=1, source_target_pairs={{0,4},{2,6},{4,0},{6,2},{1,5},{3,7},{5,1},{7,3},{8,12},{10,14},{12... | collective-permute-start | bytes 786440 | tf_op jit(solution)/shard_map/ppermute | solution.py:41
  6.3 1.5 %collective-permute-start = (bf16[128,512]{1,0:T(8,128)(2,1)S(1)}, bf16[128,512]{1,0:T(8,128)(2,1)S(1)}, u32[]{:S(2)}, u32[]{:S(2)}) collective-permute-start(bf16[128,512]{1,0:T(8,128)(2,1)S(1)} %get-tuple-element.14.refs_0_), channel_id=1, source_target_pairs={{0,2},{2,0},{4,6},{6,4},{1,3},{3,1},{5,7},{7,5},{8,10},{10,8},{12,... | collective-permute-start | bytes 393224 | tf_op jit(solution)/shard_map/ppermute | solution.py:41
  7.8 5.4 %collective-permute-done.3.refs_0_ = bf16[256,512]{1,0:T(8,128)(2,1)S(1)} collective-permute-done((bf16[256,512]{1,0:T(8,128)(2,1)S(1)}, bf16[256,512]{1,0:T(8,128)(2,1)S(1)}, u32[]{:S(2)}, u32[]{:S(2)}) %collective-permute-start.3) | collective-permute-done | bytes 262176 | tf_op jit(solution)/shard_map/ppermute | solution.py:37
  13.2 1.6 %collective-permute-start.4 = (bf16[256,512]{1,0:T(8,128)(2,1)S(1)}, bf16[256,512]{1,0:T(8,128)(2,1)S(1)}, u32[]{:S(2)}, u32[]{:S(2)}) collective-permute-start(bf16[256,512]{1,0:T(8,128)(2,1)S(1)} %collective-permute-done.3.refs_0_), channel_id=1, source_target_pairs={{0,2},{2,0},{4,6},{6,4},{1,3},{3,1},{5,7},{7,5},{8,10},{10,8},{12,... | collective-permute-start | bytes 786440 | tf_op jit(solution)/shard_map/ppermute | solution.py:41
  14.8 1.5 %collective-permute-start.1 = (bf16[64,512]{1,0:T(8,128)(2,1)S(1)}, bf16[64,512]{1,0:T(8,128)(2,1)S(1)}, u32[]{:S(2)}, u32[]{:S(2)}) collective-permute-start(bf16[64,512]{1,0:T(8,128)(2,1)S(1)} %get-tuple-element.15), channel_id=1, source_target_pairs={{0,4},{2,6},{4,0},{6,2},{1,5},{3,7},{5,1},{7,3},{8,12},{10,14},{12... | collective-permute-start | bytes 196616 | tf_op jit(solution)/shard_map/ppermute | solution.py:41
  16.3 0.3 collective-permute-start.2
  16.7 2.4 %collective-permute-done.1.refs_2_ = bf16[64,512]{1,0:T(8,128)(2,1)S(1)} collective-permute-done((bf16[64,512]{1,0:T(8,128)(2,1)S(1)}, bf16[64,512]{1,0:T(8,128)(2,1)S(1)}, u32[]{:S(2)}, u32[]{:S(2)}) %collective-permute-start.1) | collective-permute-done | bytes 65568 | tf_op jit(solution)/shard_map/ppermute | solution.py:41
  19.1 1.8 %collective-permute-start.7 = (bf16[256,512]{1,0:T(8,128)(2,1)S(1)}, bf16[256,512]{1,0:T(8,128)(2,1)S(1)}, u32[]{:S(2)}, u32[]{:S(2)}) collective-permute-start(bf16[256,512]{1,0:T(8,128)(2,1)S(1)} %collective-permute-done.3.refs_0_), channel_id=1, source_target_pairs={{0,4},{2,6},{4,0},{6,2},{1,5},{3,7},{5,1},{7,3},{8,12},{10,14},{12... | collective-permute-start | bytes 786440 | tf_op jit(solution)/shard_map/ppermute | solution.py:41
  20.9 2.1 %collective-permute-done.2.refs_3_ = bf16[64,512]{1,0:T(8,128)(2,1)S(1)} collective-permute-done((bf16[64,512]{1,0:T(8,128)(2,1)S(1)}, bf16[64,512]{1,0:T(8,128)(2,1)S(1)}, u32[]{:S(2)}, u32[]{:S(2)}) %collective-permute-start.2) | collective-permute-done | bytes 65568 | tf_op jit(solution)/shard_map/ppermute | solution.py:41
  23.0 1.5 %collective-permute-start.16 = (bf16[256,512]{1,0:T(8,128)(2,1)S(1)}, bf16[256,512]{1,0:T(8,128)(2,1)S(1)}, u32[]{:S(2)}, u32[]{:S(2)}) collective-permute-start(bf16[256,512]{1,0:T(8,128)(2,1)S(1)} %get-tuple-element.21.refs_0_), channel_id=1, source_target_pairs={{0,2},{2,0},{4,6},{6,4},{1,3},{3,1},{5,7},{7,5},{8,10},{10,8},{12,... | collective-permute-start | bytes 786440 | tf_op jit(solution)/shard_map/ppermute | solution.py:41
  24.5 0.0 collective-permute-done.refs_1_
  24.5 0.0 collective-permute-start.10
  24.5 0.0 collective-permute-done.18.refs_4_
  24.5 0.6 %collective-permute-start.20 = (bf16[256,512]{1,0:T(8,128)(2,1)S(1)}, bf16[256,512]{1,0:T(8,128)(2,1)S(1)}, u32[]{:S(2)}, u32[]{:S(2)}) collective-permute-start(bf16[256,512]{1,0:T(8,128)(2,1)S(1)} %collective-permute-done.18.refs_4_), channel_id=1, source_target_pairs={{0,2},{2,0},{4,6},{6,4},{1,3},{3,1},{5,7},{7,5},{8,10},{10,8},{12,... | collective-permute-start | bytes 786440 | tf_op jit(solution)/shard_map/ppermute | solution.py:41
  25.1 0.0 collective-permute-done.4.refs_2_
  25.1 0.2 collective-permute-start.11
  25.2 1.6 %fetch.1 = (bf16[128,4096]{1,0:T(8,128)(2,1)S(1)}, bf16[128,4096]{1,0:T(8,128)(2,1)S(1)}) custom-call(bf16[128,4096]{1,0:T(8,128)(2,1)} %bitcast.9, bf16[128,4096]{1,0:T(8,128)(2,1)} %bitcast.10), custom_call_target="tpu_custom_call" | custom-call | tf_op jit(solution)/shard_map/fetch/pallas_call | solution.py:120
  26.8 3.0 %attend.1 = (bf16[128,4096]{1,0:T(8,128)(2,1)S(1)}, f32[128,128]{1,0:T(8,128)S(1)}, bf16[128,2048]{1,0:T(8,128)(2,1)S(1)}, bf16[128,2048]{1,0:T(8,128)(2,1)S(1)}) custom-call(s32[1,8]{1,0:T(1,128)} %bitcast.15, bf16[128,4096]{1,0:T(8,128)(2,1)S(1)} %get-tuple-element.12.query_ref, bf16[128,4096]{1,0:T(8,128)(2,1)S(1)} %get-tuple-element.13.residual_ref, ...), custom_call_target="tpu_custom_call" | custom-call | tf_op jit(solution)/shard_map/attend/pallas_call | solution.py:247
  29.9 0.0 collective-permute-done.7.refs_4_
  29.9 0.7 %collective-permute-start.5 = (bf16[128,512]{1,0:T(8,128)(2,1)S(1)}, bf16[128,512]{1,0:T(8,128)(2,1)S(1)}, u32[]{:S(2)}, u32[]{:S(2)}) collective-permute-start(bf16[128,512]{1,0:T(8,128)(2,1)S(1)} %slice.8), channel_id=1, source_target_pairs={{0,4},{2,6},{4,0},{6,2},{1,5},{3,7},{5,1},{7,3},{8,12},{10,14},{12... | collective-permute-start | bytes 393224 | tf_op jit(solution)/shard_map/ppermute | solution.py:41
  30.6 0.5 collective-permute-done.16.refs_2_
  31.1 0.0 collective-permute-start.12
  31.1 0.0 collective-permute-done.10.refs_1_
  31.1 2.5 %collective-permute-start.8 = (bf16[128,512]{1,0:T(8,128)(2,1)S(1)}, bf16[128,512]{1,0:T(8,128)(2,1)S(1)}, u32[]{:S(2)}, u32[]{:S(2)}) collective-permute-start(bf16[128,512]{1,0:T(8,128)(2,1)S(1)} %slice.9), channel_id=1, source_target_pairs={{0,2},{2,0},{4,6},{6,4},{1,3},{3,1},{5,7},{7,5},{8,10},{10,8},{12,... | collective-permute-start | bytes 393224 | tf_op jit(solution)/shard_map/ppermute | solution.py:41
  33.6 1.4 %collective-permute-done.20.refs_6_ = bf16[256,512]{1,0:T(8,128)(2,1)S(1)} collective-permute-done((bf16[256,512]{1,0:T(8,128)(2,1)S(1)}, bf16[256,512]{1,0:T(8,128)(2,1)S(1)}, u32[]{:S(2)}, u32[]{:S(2)}) %collective-permute-start.20) | collective-permute-done | bytes 262176 | tf_op jit(solution)/shard_map/ppermute | solution.py:41
  35.0 3.5 %collective-permute-start.14 = (bf16[128,2048]{1,0:T(8,128)(2,1)S(1)}, bf16[128,2048]{1,0:T(8,128)(2,1)S(1)}, u32[]{:S(2)}, u32[]{:S(2)}) collective-permute-start(bf16[128,2048]{1,0:T(8,128)(2,1)S(1)} %get-tuple-element.20), channel_id=1, source_target_pairs={{0,8},{8,16},{16,24},{1,9},{9,17},{17,25},{2,10},{10,18},{18,26},{... | collective-permute-start | bytes 1572872 | tf_op jit(solution)/shard_map/ppermute | solution.py:37
  38.5 0.0 collective-permute-done.5.refs_0_
  38.5 0.1 collective-permute-start.6
  38.6 0.0 collective-permute-done.8.refs_2_
  38.6 0.5 collective-permute-start.9
  39.1 0.0 collective-permute-done.11.refs_3_
  39.1 0.1 collective-permute-start.15
  39.2 0.0 collective-permute-done.12.refs_5_
  39.2 0.4 collective-permute-start.19
  39.6 0.3 collective-permute-done.6.refs_1_
  39.9 0.1 collective-permute-start.17
  40.1 0.0 collective-permute-done.9.refs_3_
  40.1 0.3 collective-permute-start.21
  40.4 0.4 project.3.refs_4_
  40.8 0.3 project.4
  41.1 0.0 collective-permute-done.15.refs_1_
  41.1 3.5 %collective-permute-start.13 = (bf16[128,512]{1,0:T(8,128)(2,1)S(1)}, bf16[128,512]{1,0:T(8,128)(2,1)S(1)}, u32[]{:S(2)}, u32[]{:S(2)}) collective-permute-start(bf16[128,512]{1,0:T(8,128)(2,1)S(1)} %project.4), channel_id=1, source_target_pairs={{0,8},{8,16},{16,24},{1,9},{9,17},{17,25},{2,10},{10,18},{18,26},{... | collective-permute-start | bytes 393224 | tf_op jit(solution)/shard_map/ppermute | solution.py:37
  44.6 1.0 %store.1 = bf16[128,4096]{1,0:T(8,128)(2,1)} custom-call(bf16[128,4096]{1,0:T(8,128)(2,1)S(1)} %get-tuple-element.16.near_ref), custom_call_target="tpu_custom_call" | custom-call | tf_op jit(solution)/shard_map/store/pallas_call | solution.py:136
  45.6 0.0 collective-permute-done.19.refs_5_
  45.6 0.0 collective-permute-done.17.refs_3_
  45.6 4.4 %collective-permute-done.14.layer_ref = bf16[128,2048]{1,0:T(8,128)(2,1)S(1)} collective-permute-done((bf16[128,2048]{1,0:T(8,128)(2,1)S(1)}, bf16[128,2048]{1,0:T(8,128)(2,1)S(1)}, u32[]{:S(2)}, u32[]{:S(2)}) %collective-permute-start.14) | collective-permute-done | bytes 524320 | tf_op jit(solution)/shard_map/ppermute | solution.py:37
  50.0 0.0 collective-permute-done.21.refs_7_
  50.0 0.5 project.5
  50.5 0.9 %collective-permute-done.13 = bf16[128,512]{1,0:T(8,128)(2,1)S(1)} collective-permute-done((bf16[128,512]{1,0:T(8,128)(2,1)S(1)}, bf16[128,512]{1,0:T(8,128)(2,1)S(1)}, u32[]{:S(2)}, u32[]{:S(2)}) %collective-permute-start.13) | collective-permute-done | bytes 131104 | tf_op jit(solution)/shard_map/ppermute | solution.py:37
  51.4 0.7 %fusion = bf16[1,1,128,512]{3,2,1,0:T(8,128)(2,1)} fusion(f32[128,512]{1,0:T(8,128)S(1)} %project.5, bf16[128,512]{1,0:T(8,128)(2,1)S(1)} %collective-permute-done.13), kind=kLoop, calls=%fused_computation.1 | loop fusion | flops 196608 | bytes 524288 | tf_op jit(solution)/shard_map/broadcast_in_dim | solution.py:366
  (2 shorter events, 0.0 us)
Async XLA Ops:
  1.9 11.3 %collective-permute-start.3 = (bf16[256,512]{1,0:T(8,128)(2,1)S(1)}, bf16[256,512]{1,0:T(8,128)(2,1)S(1)}, u32[]{:S(2)}, u32[]{:S(2)}) collective-permute-start(bf16[256,512]{1,0:T(8,128)(2,1)S(1)} %get-tuple-element.18), channel_id=1, source_target_pairs={{8,0},{16,8},{24,16},{9,1},{17,9},{25,17},{10,2},{18,10},{26,18},{... | collective-permute-start | bytes 786440 | tf_op jit(solution)/shard_map/ppermute | solution.py:37
  3.2 21.3 %collective-permute-start.18 = (bf16[256,512]{1,0:T(8,128)(2,1)S(1)}, bf16[256,512]{1,0:T(8,128)(2,1)S(1)}, u32[]{:S(2)}, u32[]{:S(2)}) collective-permute-start(bf16[256,512]{1,0:T(8,128)(2,1)S(1)} %get-tuple-element.21.refs_0_), channel_id=1, source_target_pairs={{0,4},{2,6},{4,0},{6,2},{1,5},{3,7},{5,1},{7,3},{8,12},{10,14},{12... | collective-permute-start | bytes 786440 | tf_op jit(solution)/shard_map/ppermute | solution.py:41
  6.3 18.2 %collective-permute-start = (bf16[128,512]{1,0:T(8,128)(2,1)S(1)}, bf16[128,512]{1,0:T(8,128)(2,1)S(1)}, u32[]{:S(2)}, u32[]{:S(2)}) collective-permute-start(bf16[128,512]{1,0:T(8,128)(2,1)S(1)} %get-tuple-element.14.refs_0_), channel_id=1, source_target_pairs={{0,2},{2,0},{4,6},{6,4},{1,3},{3,1},{5,7},{7,5},{8,10},{10,8},{12,... | collective-permute-start | bytes 393224 | tf_op jit(solution)/shard_map/ppermute | solution.py:41
  13.2 11.9 %collective-permute-start.4 = (bf16[256,512]{1,0:T(8,128)(2,1)S(1)}, bf16[256,512]{1,0:T(8,128)(2,1)S(1)}, u32[]{:S(2)}, u32[]{:S(2)}) collective-permute-start(bf16[256,512]{1,0:T(8,128)(2,1)S(1)} %collective-permute-done.3.refs_0_), channel_id=1, source_target_pairs={{0,2},{2,0},{4,6},{6,4},{1,3},{3,1},{5,7},{7,5},{8,10},{10,8},{12,... | collective-permute-start | bytes 786440 | tf_op jit(solution)/shard_map/ppermute | solution.py:41
  14.8 4.3 %collective-permute-start.1 = (bf16[64,512]{1,0:T(8,128)(2,1)S(1)}, bf16[64,512]{1,0:T(8,128)(2,1)S(1)}, u32[]{:S(2)}, u32[]{:S(2)}) collective-permute-start(bf16[64,512]{1,0:T(8,128)(2,1)S(1)} %get-tuple-element.15), channel_id=1, source_target_pairs={{0,4},{2,6},{4,0},{6,2},{1,5},{3,7},{5,1},{7,3},{8,12},{10,14},{12... | collective-permute-start | bytes 196616 | tf_op jit(solution)/shard_map/ppermute | solution.py:41
  16.3 6.6 %collective-permute-start.2 = (bf16[64,512]{1,0:T(8,128)(2,1)S(1)}, bf16[64,512]{1,0:T(8,128)(2,1)S(1)}, u32[]{:S(2)}, u32[]{:S(2)}) collective-permute-start(bf16[64,512]{1,0:T(8,128)(2,1)S(1)} %get-tuple-element.15), channel_id=1, source_target_pairs={{0,6},{2,4},{4,2},{6,0},{1,7},{3,5},{5,3},{7,1},{8,14},{10,12},{12... | collective-permute-start | bytes 196616 | tf_op jit(solution)/shard_map/ppermute | solution.py:41
  19.1 10.8 %collective-permute-start.7 = (bf16[256,512]{1,0:T(8,128)(2,1)S(1)}, bf16[256,512]{1,0:T(8,128)(2,1)S(1)}, u32[]{:S(2)}, u32[]{:S(2)}) collective-permute-start(bf16[256,512]{1,0:T(8,128)(2,1)S(1)} %collective-permute-done.3.refs_0_), channel_id=1, source_target_pairs={{0,4},{2,6},{4,0},{6,2},{1,5},{3,7},{5,1},{7,3},{8,12},{10,14},{12... | collective-permute-start | bytes 786440 | tf_op jit(solution)/shard_map/ppermute | solution.py:41
  23.0 8.1 %collective-permute-start.16 = (bf16[256,512]{1,0:T(8,128)(2,1)S(1)}, bf16[256,512]{1,0:T(8,128)(2,1)S(1)}, u32[]{:S(2)}, u32[]{:S(2)}) collective-permute-start(bf16[256,512]{1,0:T(8,128)(2,1)S(1)} %get-tuple-element.21.refs_0_), channel_id=1, source_target_pairs={{0,2},{2,0},{4,6},{6,4},{1,3},{3,1},{5,7},{7,5},{8,10},{10,8},{12,... | collective-permute-start | bytes 786440 | tf_op jit(solution)/shard_map/ppermute | solution.py:41
  24.5 6.6 %collective-permute-start.10 = (bf16[256,512]{1,0:T(8,128)(2,1)S(1)}, bf16[256,512]{1,0:T(8,128)(2,1)S(1)}, u32[]{:S(2)}, u32[]{:S(2)}) collective-permute-start(bf16[256,512]{1,0:T(8,128)(2,1)S(1)} %collective-permute-done.3.refs_0_), channel_id=1, source_target_pairs={{0,1},{1,0},{2,3},{3,2},{4,5},{5,4},{6,7},{7,6},{8,9},{9,8},{10,11... | collective-permute-start | bytes 786440 | tf_op jit(solution)/shard_map/ppermute | solution.py:41
  24.5 10.5 %collective-permute-start.20 = (bf16[256,512]{1,0:T(8,128)(2,1)S(1)}, bf16[256,512]{1,0:T(8,128)(2,1)S(1)}, u32[]{:S(2)}, u32[]{:S(2)}) collective-permute-start(bf16[256,512]{1,0:T(8,128)(2,1)S(1)} %collective-permute-done.18.refs_4_), channel_id=1, source_target_pairs={{0,2},{2,0},{4,6},{6,4},{1,3},{3,1},{5,7},{7,5},{8,10},{10,8},{12,... | collective-permute-start | bytes 786440 | tf_op jit(solution)/shard_map/ppermute | solution.py:41
  25.1 14.0 %collective-permute-start.11 = (bf16[256,512]{1,0:T(8,128)(2,1)S(1)}, bf16[256,512]{1,0:T(8,128)(2,1)S(1)}, u32[]{:S(2)}, u32[]{:S(2)}) collective-permute-start(bf16[256,512]{1,0:T(8,128)(2,1)S(1)} %collective-permute-done.4.refs_2_), channel_id=1, source_target_pairs={{0,1},{1,0},{2,3},{3,2},{4,5},{5,4},{6,7},{7,6},{8,9},{9,8},{10,11... | collective-permute-start | bytes 786440 | tf_op jit(solution)/shard_map/ppermute | solution.py:41
  29.9 8.6 %collective-permute-start.5 = (bf16[128,512]{1,0:T(8,128)(2,1)S(1)}, bf16[128,512]{1,0:T(8,128)(2,1)S(1)}, u32[]{:S(2)}, u32[]{:S(2)}) collective-permute-start(bf16[128,512]{1,0:T(8,128)(2,1)S(1)} %slice.8), channel_id=1, source_target_pairs={{0,4},{2,6},{4,0},{6,2},{1,5},{3,7},{5,1},{7,3},{8,12},{10,14},{12... | collective-permute-start | bytes 393224 | tf_op jit(solution)/shard_map/ppermute | solution.py:41
  31.1 8.1 %collective-permute-start.12 = (bf16[256,512]{1,0:T(8,128)(2,1)S(1)}, bf16[256,512]{1,0:T(8,128)(2,1)S(1)}, u32[]{:S(2)}, u32[]{:S(2)}) collective-permute-start(bf16[256,512]{1,0:T(8,128)(2,1)S(1)} %collective-permute-done.7.refs_4_), channel_id=1, source_target_pairs={{0,1},{1,0},{2,3},{3,2},{4,5},{5,4},{6,7},{7,6},{8,9},{9,8},{10,11... | collective-permute-start | bytes 786440 | tf_op jit(solution)/shard_map/ppermute | solution.py:41
  31.1 7.5 %collective-permute-start.8 = (bf16[128,512]{1,0:T(8,128)(2,1)S(1)}, bf16[128,512]{1,0:T(8,128)(2,1)S(1)}, u32[]{:S(2)}, u32[]{:S(2)}) collective-permute-start(bf16[128,512]{1,0:T(8,128)(2,1)S(1)} %slice.9), channel_id=1, source_target_pairs={{0,2},{2,0},{4,6},{6,4},{1,3},{3,1},{5,7},{7,5},{8,10},{10,8},{12,... | collective-permute-start | bytes 393224 | tf_op jit(solution)/shard_map/ppermute | solution.py:41
  35.0 15.0 %collective-permute-start.14 = (bf16[128,2048]{1,0:T(8,128)(2,1)S(1)}, bf16[128,2048]{1,0:T(8,128)(2,1)S(1)}, u32[]{:S(2)}, u32[]{:S(2)}) collective-permute-start(bf16[128,2048]{1,0:T(8,128)(2,1)S(1)} %get-tuple-element.20), channel_id=1, source_target_pairs={{0,8},{8,16},{16,24},{1,9},{9,17},{17,25},{2,10},{10,18},{18,26},{... | collective-permute-start | bytes 1572872 | tf_op jit(solution)/shard_map/ppermute | solution.py:37
  38.5 1.4 %collective-permute-start.6 = (bf16[128,512]{1,0:T(8,128)(2,1)S(1)}, bf16[128,512]{1,0:T(8,128)(2,1)S(1)}, u32[]{:S(2)}, u32[]{:S(2)}) collective-permute-start(bf16[128,512]{1,0:T(8,128)(2,1)S(1)} %collective-permute-done.5.refs_0_), channel_id=1, source_target_pairs={{0,1},{1,0},{2,3},{3,2},{4,5},{5,4},{6,7},{7,6},{8,9},{9,8},{10,11... | collective-permute-start | bytes 393224 | tf_op jit(solution)/shard_map/ppermute | solution.py:41
  38.6 1.5 %collective-permute-start.9 = (bf16[128,512]{1,0:T(8,128)(2,1)S(1)}, bf16[128,512]{1,0:T(8,128)(2,1)S(1)}, u32[]{:S(2)}, u32[]{:S(2)}) collective-permute-start(bf16[128,512]{1,0:T(8,128)(2,1)S(1)} %collective-permute-done.8.refs_2_), channel_id=1, source_target_pairs={{0,1},{1,0},{2,3},{3,2},{4,5},{5,4},{6,7},{7,6},{8,9},{9,8},{10,11... | collective-permute-start | bytes 393224 | tf_op jit(solution)/shard_map/ppermute | solution.py:41
  39.1 2.0 %collective-permute-start.15 = (bf16[256,512]{1,0:T(8,128)(2,1)S(1)}, bf16[256,512]{1,0:T(8,128)(2,1)S(1)}, u32[]{:S(2)}, u32[]{:S(2)}) collective-permute-start(bf16[256,512]{1,0:T(8,128)(2,1)S(1)} %get-tuple-element.21.refs_0_), channel_id=1, source_target_pairs={{0,1},{1,0},{2,3},{3,2},{4,5},{5,4},{6,7},{7,6},{8,9},{9,8},{10,11... | collective-permute-start | bytes 786440 | tf_op jit(solution)/shard_map/ppermute | solution.py:41
  39.2 6.4 %collective-permute-start.19 = (bf16[256,512]{1,0:T(8,128)(2,1)S(1)}, bf16[256,512]{1,0:T(8,128)(2,1)S(1)}, u32[]{:S(2)}, u32[]{:S(2)}) collective-permute-start(bf16[256,512]{1,0:T(8,128)(2,1)S(1)} %collective-permute-done.18.refs_4_), channel_id=1, source_target_pairs={{0,1},{1,0},{2,3},{3,2},{4,5},{5,4},{6,7},{7,6},{8,9},{9,8},{10,11... | collective-permute-start | bytes 786440 | tf_op jit(solution)/shard_map/ppermute | solution.py:41
  39.9 5.7 %collective-permute-start.17 = (bf16[256,512]{1,0:T(8,128)(2,1)S(1)}, bf16[256,512]{1,0:T(8,128)(2,1)S(1)}, u32[]{:S(2)}, u32[]{:S(2)}) collective-permute-start(bf16[256,512]{1,0:T(8,128)(2,1)S(1)} %collective-permute-done.16.refs_2_), channel_id=1, source_target_pairs={{0,1},{1,0},{2,3},{3,2},{4,5},{5,4},{6,7},{7,6},{8,9},{9,8},{10,11... | collective-permute-start | bytes 786440 | tf_op jit(solution)/shard_map/ppermute | solution.py:41
  40.1 9.9 %collective-permute-start.21 = (bf16[256,512]{1,0:T(8,128)(2,1)S(1)}, bf16[256,512]{1,0:T(8,128)(2,1)S(1)}, u32[]{:S(2)}, u32[]{:S(2)}) collective-permute-start(bf16[256,512]{1,0:T(8,128)(2,1)S(1)} %collective-permute-done.20.refs_6_), channel_id=1, source_target_pairs={{0,1},{1,0},{2,3},{3,2},{4,5},{5,4},{6,7},{7,6},{8,9},{9,8},{10,11... | collective-permute-start | bytes 786440 | tf_op jit(solution)/shard_map/ppermute | solution.py:41
  41.1 10.3 %collective-permute-start.13 = (bf16[128,512]{1,0:T(8,128)(2,1)S(1)}, bf16[128,512]{1,0:T(8,128)(2,1)S(1)}, u32[]{:S(2)}, u32[]{:S(2)}) collective-permute-start(bf16[128,512]{1,0:T(8,128)(2,1)S(1)} %project.4), channel_id=1, source_target_pairs={{0,8},{8,16},{16,24},{1,9},{9,17},{17,25},{2,10},{10,18},{18,26},{... | collective-permute-start | bytes 393224 | tf_op jit(solution)/shard_map/ppermute | solution.py:37

commit v2 on v1

--- a/solution.py
+++ b/solution.py
@@ -14,6 +14,7 @@
 
 epsilon = 1e-06
 MASKED = -1e30
+FEWER = 96
 
 WHOLE = pl.BlockSpec(memory_space=pltpu.VMEM)
 FAR = pl.BlockSpec(memory_space=pltpu.HBM)
@@ -35,6 +36,17 @@
     devices = range(lax.axis_size("pipe"))
     route = [(i - distance, i) for i in devices if i - distance in devices]
     return lax.ppermute(block, "pipe", route)
+
+
+def paired(block, first):
+    sections, cores = lax.axis_size("pipe"), lax.axis_size("exp")
+    route = []
+    for section in range(sections):
+        other = section + 1 if (section - first) % 2 == 0 else section - 1
+        for core in range(cores):
+            target = other * cores + core if 0 <= other < sections else section * cores + (core ^ 1)
+            route.append((section * cores + core, target))
+    return lax.ppermute(block, ("pipe", "exp"), route)
 
 
 def exchanged(block, axis, bit):
@@ -263,18 +275,25 @@
     )(far(lengths), *[near(array) for array in (queries, residual, *pairs)])
 
 
-def project_kernel(places, scaled, layer_ref, *refs):
+def project_kernel(places, scaled, sides, *refs):
+    layer_refs, refs = refs[:sides], refs[sides:]
+    layer_ref = layer_refs[0]
+    odd = lax.axis_index("pipe") % 2 == 1
     piece_refs = refs[: len(places)]
     *rest, out_ref = refs[len(places) :]
     depth = layer_ref.shape[1] // (lax.axis_size("seq") * lax.axis_size("exp"))
     seq, core = lax.axis_index("seq"), lax.axis_index("exp")
     total = rest[0][...] if len(rest) > scaled else None
-    for (bit, kind, first), piece_ref in zip(places, piece_refs):
-        rows = piece_ref.shape[0]
-        column = ((seq ^ bit) * 2 + (core ^ kind)) * depth + first
-        part = jnp.dot(
-            layer_ref[:, pl.ds(pl.multiple_of(column, DH), rows)], piece_ref[...], preferred_element_type=jnp.float32
-        )
+    blocks = {}
+    for (bit, kind, _), piece_ref in zip(places, piece_refs):
+        blocks.setdefault((bit, kind), []).append(piece_ref[...])
+    for (bit, kind), pieces in blocks.items():
+        column = ((seq ^ bit) * 2 + (core ^ kind)) * depth
+        cols = pl.ds(pl.multiple_of(column, DH), depth)
+        block = layer_ref[:, cols]
+        if sides == 2:
+            block = jnp.where(odd, block, layer_refs[1][:, cols])
+        part = jnp.dot(block, jnp.concatenate(pieces, axis=0), preferred_element_type=jnp.float32)
         total = part if total is None else total + part
     if scaled:
         for left in range(0, total.shape[1], DH):
@@ -285,19 +304,44 @@
 
 
 def project(layer, held, so_far=None, inverse=None):
-    places = tuple(held)
+    layers = layer if isinstance(layer, list) else [layer]
+    places = tuple(sorted(held))
     scaled = inverse is not None
     blocks = [held[place] for place in places]
     extra = [array for array in (so_far, inverse) if array is not None]
-    shape = (layer.shape[0], blocks[0].shape[1])
-    return pl.pallas_call(
-        functools.partial(project_kernel, places, scaled),
+    shape = (layers[0].shape[0], blocks[0].shape[1])
+    return pl.pallas_call(
+        functools.partial(project_kernel, places, scaled, len(layers)),
         out_shape=pltpu.VMEM(shape, jnp.bfloat16 if scaled else jnp.float32),
-        in_specs=[WHOLE] * (1 + len(blocks) + len(extra)),
+        in_specs=[WHOLE] * (len(layers) + len(blocks) + len(extra)),
         out_specs=WHOLE,
         compiler_params=budget(8),
         name="project",
-    )(*[near(array) for array in (layer, *blocks, *extra)])
+    )(*[near(array) for array in (*layers, *blocks, *extra)])
+
+
+def finish_kernel(total_ref, *refs):
+    *arrived_refs, far_ref, near_ref, sem = refs
+    section = lax.axis_index("pipe")
+    arrived = arrived_refs[0][...].astype(jnp.float32)
+    if len(arrived_refs) == 2:
+        arrived = jnp.where(section % 2 == 1, arrived, arrived_refs[1][...].astype(jnp.float32))
+    summed = (arrived + total_ref[...]).astype(jnp.bfloat16)
+    near_ref[...] = jnp.where(section > 0, summed, jnp.zeros_like(summed))
+    run_copies([pltpu.make_async_copy(near_ref, far_ref, sem)])
+
+
+def finish(total, *arrived):
+    shape = jax.ShapeDtypeStruct(total.shape, jnp.bfloat16)
+    return pl.pallas_call(
+        finish_kernel,
+        out_shape=shape,
+        in_specs=[WHOLE] * (1 + len(arrived)),
+        out_specs=FAR,
+        scratch_shapes=[pltpu.VMEM(shape.shape, shape.dtype), pltpu.SemaphoreType.DMA],
+        compiler_params=budget(2),
+        name="finish",
+    )(*[near(array) for array in (total, *arrived)])
 
 
 def gather_square(block, relays):
@@ -312,19 +356,20 @@
     for bit in (1, 2):
         sides[bit] = exchanged(block, "seq", bit)
         hold(early, bit, 0, sides[bit])
-    part = block.shape[0] // len(relays)
-    for index, bit in enumerate(relays):
-        start = index * part
-        corner = exchanged(sides[bit][start : start + part], "seq", 3 - bit)
+    start = 0
+    for bit, rows in relays:
+        corner = exchanged(sides[bit][start : start + rows], "seq", 3 - bit)
         hold(late, 3, start, corner)
+        start += rows
     return early, late
 
 
 def square_of_chips(queries, key_rows, value_rows, residual, lengths, norm_gain, weight):
     pair, half, leaves, stays = prepare(key_rows, value_rows, norm_gain, weight, 2)
     leaves = shifted(leaves, -1)
-    leaves_early, leaves_late = gather_square(leaves, (1, 2))
-    stays_early, stays_late = gather_square(stays, (2,))
+    rows = leaves.shape[0]
+    leaves_early, leaves_late = gather_square(leaves, ((1, rows - FEWER), (2, FEWER)))
+    stays_early, stays_late = gather_square(stays, ((2, rows),))
     pairs = [pair, exchanged(pair, "seq", 1)]
     pairs.append(exchanged(half, "seq", 2))
     pairs.append(exchanged(half, "seq", 3))
@@ -336,12 +381,16 @@
         lengths, queries, residual, pairs, lax.axis_size("seq"), parts
     )
     context = store(context)
-    received = shifted(normed, 1)
+    received = []
+    for first in (0, 1):
+        received.append(paired(normed, first))
     so_far = project(layer, leaves_early)
     projected = project(layer, leaves_late, so_far, inverse)
-    arrived = shifted(projected, 1)
+    arrived = []
+    for first in (0, 1):
+        arrived.append(paired(projected, first))
     total = project(received, {**stays_early, **stays_late})
-    return context, (arrived.astype(jnp.float32) + total).astype(jnp.bfloat16)
+    return context, finish(total, *arrived)
 
 
 def any_mesh(queries, key_rows, value_rows, residual, lengths, norm_gain, weight):

time: 52.3 us -> 60.9 us (1.16)
  waiting for transfers between devices: 17.6 us -> 31.3 us
  starting transfers between devices: 25.1 us -> 20 us
  other arithmetic: 0.68 us -> 0 us
  Pallas kernels: 7.99 us -> 8.67 us
    ppermute x0 -> x4, waiting for transfers between devices: none -> 9.59 us  [paired(): return lax.ppermute(block, ('pipe', 'exp'), route)]
    ppermute x19, waiting for transfers between devices: 6.85 us -> 14.8 us  [exchanged(): lax.ppermute(block, axis, [(i, i ^ bit) for i in range(lax.axis_size(axis...]
    ppermute x3 -> x1, starting transfers between devices: 8.27 us -> 1.29 us  [shifted(): return lax.ppermute(block, 'pipe', route)]
    ppermute x3 -> x1, waiting for transfers between devices: 10.7 us -> 6.9 us  [shifted(): return lax.ppermute(block, 'pipe', route)]
    ppermute x0 -> x4, starting transfers between devices: none -> 2.87 us  [paired(): return lax.ppermute(block, ('pipe', 'exp'), route)]
    ppermute x19, starting transfers between devices: 16.8 us -> 15.9 us  [exchanged(): lax.ppermute(block, axis, [(i, i ^ bit) for i in range(lax.axis_size(axis...]
    pallas_call x3 -> x4, Pallas kernels: 1.14 us -> 1.82 us  [the longest x3 1.1 us: project(): pl.pallas_call(functools.partial(project_kernel, places, scaled, len(laye...]
    broadcast_in_dim x1 -> x0, other arithmetic: 0.68 us -> none  [on_device(): return (context[None, None], kv_next[None, None])]
  transfers between devices with their start and end apart: 22 -> 24, of which waited for: 8 -> 9; matrix products, arithmetic and copies ran while one was open for 0% -> 0% of each run, Pallas kernels for 13% -> 11%
where the time goes in v2:
time: 60.9 us; the launch traced here: 60.7 us
  waiting for transfers between devices  31.3 us (51%)
  starting transfers between devices  20 us (33%)
  Pallas kernels  8.67 us (14%)
  between operations  0.75 us (1%)
    ppermute x19, starting transfers between devices, exchanged(): lax.ppermute(block, axis, [(i, i ^ bit) for i in range(lax.axis_size(axis...  15.9 us
    ppermute x19, waiting for transfers between devices, exchanged(): lax.ppermute(block, axis, [(i, i ^ bit) for i in range(lax.axis_size(axis...  14.8 us
    ppermute x4, waiting for transfers between devices, paired(): return lax.ppermute(block, ('pipe', 'exp'), route)  9.59 us
    ppermute x1, waiting for transfers between devices, shifted(): return lax.ppermute(block, 'pipe', route)  6.9 us
    pallas_call x1, Pallas kernels, attend(): pl.pallas_call(functools.partial(attend_kernel, groups, longest, 1.0 / ma...  3.04 us
    ppermute x4, starting transfers between devices, paired(): return lax.ppermute(block, ('pipe', 'exp'), route)  2.87 us
    pallas_call x1, Pallas kernels, fetch(): pl.pallas_call(fetch_kernel, out_shape=tuple((pltpu.VMEM(array.shape, arr...  1.56 us
    ppermute x1, starting transfers between devices, shifted(): return lax.ppermute(block, 'pipe', route)  1.29 us
  transfers between devices with their start and end apart: 24, of which 9 were waited for; matrix products, arithmetic and copies ran while one was open for 0% of the time, Pallas kernels for 11%

profile of v2, /device:TPU:0, one launch (start us, length us, event | category | flops | bytes accessed | tf_op | source)
XLA Modules:
  0.0 60.7 jit_solution(17756161907152272201)
XLA Ops:
  0.6 1.3 %prepare.1 = (bf16[128,512]{1,0:T(8,128)(2,1)S(1)}, bf16[64,512]{1,0:T(8,128)(2,1)S(1)}, bf16[256,512]{1,0:T(8,128)(2,1)S(1)}, bf16[256,512]{1,0:T(8,128)(2,1)S(1)}) custom-call(bf16[128,256]{1,0:T(8,128)(2,1)} %bitcast.13, bf16[128,256]{1,0:T(8,128)(2,1)} %bitcast.14, f32[1,4096]{1,0:T(1,128)} %gain_ref.1, bf16[512,512]{1,0:T(8,128)(2,1)} %bitcast.11), custom_call_target="tpu_custom_call" | custom-call | tf_op jit(solution)/shard_map/prepare/pallas_call | solution.py:104
  1.9 1.3 %collective-permute-start.12 = (bf16[256,512]{1,0:T(8,128)(2,1)S(1)}, bf16[256,512]{1,0:T(8,128)(2,1)S(1)}, u32[]{:S(2)}, u32[]{:S(2)}) collective-permute-start(bf16[256,512]{1,0:T(8,128)(2,1)S(1)} %get-tuple-element.20), channel_id=1, source_target_pairs={{8,0},{16,8},{24,16},{9,1},{17,9},{25,17},{10,2},{18,10},{26,18},{... | collective-permute-start | bytes 786440 | tf_op jit(solution)/shard_map/ppermute | solution.py:38
  3.2 3.1 %collective-permute-start.8 = (bf16[256,512]{1,0:T(8,128)(2,1)S(1)}, bf16[256,512]{1,0:T(8,128)(2,1)S(1)}, u32[]{:S(2)}, u32[]{:S(2)}) collective-permute-start(bf16[256,512]{1,0:T(8,128)(2,1)S(1)} %get-tuple-element.18.refs_2_), channel_id=1, source_target_pairs={{0,4},{2,6},{4,0},{6,2},{1,5},{3,7},{5,1},{7,3},{8,12},{10,14},{12... | collective-permute-start | bytes 786440 | tf_op jit(solution)/shard_map/ppermute | solution.py:53
  6.3 6.9 %collective-permute-done.12.refs_1_ = bf16[256,512]{1,0:T(8,128)(2,1)S(1)} collective-permute-done((bf16[256,512]{1,0:T(8,128)(2,1)S(1)}, bf16[256,512]{1,0:T(8,128)(2,1)S(1)}, u32[]{:S(2)}, u32[]{:S(2)}) %collective-permute-start.12) | collective-permute-done | bytes 262176 | tf_op jit(solution)/shard_map/ppermute | solution.py:38
  13.2 1.6 %collective-permute-start.13 = (bf16[256,512]{1,0:T(8,128)(2,1)S(1)}, bf16[256,512]{1,0:T(8,128)(2,1)S(1)}, u32[]{:S(2)}, u32[]{:S(2)}) collective-permute-start(bf16[256,512]{1,0:T(8,128)(2,1)S(1)} %collective-permute-done.12.refs_1_), channel_id=1, source_target_pairs={{0,2},{2,0},{4,6},{6,4},{1,3},{3,1},{5,7},{7,5},{8,10},{10,8},{12,... | collective-permute-start | bytes 786440 | tf_op jit(solution)/shard_map/ppermute | solution.py:53
  14.8 0.4 collective-permute-start
  15.2 1.7 %collective-permute-start.1 = (bf16[64,512]{1,0:T(8,128)(2,1)S(1)}, bf16[64,512]{1,0:T(8,128)(2,1)S(1)}, u32[]{:S(2)}, u32[]{:S(2)}) collective-permute-start(bf16[64,512]{1,0:T(8,128)(2,1)S(1)} %get-tuple-element.15), channel_id=1, source_target_pairs={{0,4},{2,6},{4,0},{6,2},{1,5},{3,7},{5,1},{7,3},{8,12},{10,14},{12... | collective-permute-start | bytes 196616 | tf_op jit(solution)/shard_map/ppermute | solution.py:53
  16.9 1.4 %collective-permute-start.2 = (bf16[64,512]{1,0:T(8,128)(2,1)S(1)}, bf16[64,512]{1,0:T(8,128)(2,1)S(1)}, u32[]{:S(2)}, u32[]{:S(2)}) collective-permute-start(bf16[64,512]{1,0:T(8,128)(2,1)S(1)} %get-tuple-element.15), channel_id=1, source_target_pairs={{0,6},{2,4},{4,2},{6,0},{1,7},{3,5},{5,3},{7,1},{8,14},{10,12},{12... | collective-permute-start | bytes 196616 | tf_op jit(solution)/shard_map/ppermute | solution.py:53
  18.3 1.2 %collective-permute-done.1.refs_2_ = bf16[64,512]{1,0:T(8,128)(2,1)S(1)} collective-permute-done((bf16[64,512]{1,0:T(8,128)(2,1)S(1)}, bf16[64,512]{1,0:T(8,128)(2,1)S(1)}, u32[]{:S(2)}, u32[]{:S(2)}) %collective-permute-start.1) | collective-permute-done | bytes 65568 | tf_op jit(solution)/shard_map/ppermute | solution.py:53
  19.5 1.6 %collective-permute-start.6 = (bf16[256,512]{1,0:T(8,128)(2,1)S(1)}, bf16[256,512]{1,0:T(8,128)(2,1)S(1)}, u32[]{:S(2)}, u32[]{:S(2)}) collective-permute-start(bf16[256,512]{1,0:T(8,128)(2,1)S(1)} %get-tuple-element.18.refs_2_), channel_id=1, source_target_pairs={{0,2},{2,0},{4,6},{6,4},{1,3},{3,1},{5,7},{7,5},{8,10},{10,8},{12,... | collective-permute-start | bytes 786440 | tf_op jit(solution)/shard_map/ppermute | solution.py:53
  21.1 6.6 %collective-permute-done.2.refs_3_ = bf16[64,512]{1,0:T(8,128)(2,1)S(1)} collective-permute-done((bf16[64,512]{1,0:T(8,128)(2,1)S(1)}, bf16[64,512]{1,0:T(8,128)(2,1)S(1)}, u32[]{:S(2)}, u32[]{:S(2)}) %collective-permute-start.2) | collective-permute-done | bytes 65568 | tf_op jit(solution)/shard_map/ppermute | solution.py:53
  27.7 0.0 collective-permute-start.5
  27.7 0.0 collective-permute-done.refs_1_
  27.7 0.4 collective-permute-start.15
  28.0 0.0 collective-permute-done.8.refs_6_
  28.0 0.2 collective-permute-start.19
  28.3 0.0 collective-permute-done.13.refs_3_
  28.3 1.6 %collective-permute-start.10 = (bf16[256,512]{1,0:T(8,128)(2,1)S(1)}, bf16[256,512]{1,0:T(8,128)(2,1)S(1)}, u32[]{:S(2)}, u32[]{:S(2)}) collective-permute-start(bf16[256,512]{1,0:T(8,128)(2,1)S(1)} %collective-permute-done.8.refs_6_), channel_id=1, source_target_pairs={{0,2},{2,0},{4,6},{6,4},{1,3},{3,1},{5,7},{7,5},{8,10},{10,8},{12,... | collective-permute-start | bytes 786440 | tf_op jit(solution)/shard_map/ppermute | solution.py:53
  29.9 0.5 collective-permute-done.6.refs_4_
  30.5 1.4 %collective-permute-start.14 = (bf16[160,512]{1,0:T(8,128)(2,1)S(1)}, bf16[160,512]{1,0:T(8,128)(2,1)S(1)}, u32[]{:S(2)}, u32[]{:S(2)}) collective-permute-start(bf16[160,512]{1,0:T(8,128)(2,1)S(1)} %slice.8), channel_id=1, source_target_pairs={{0,4},{2,6},{4,0},{6,2},{1,5},{3,7},{5,1},{7,3},{8,12},{10,14},{12... | collective-permute-start | bytes 491528 | tf_op jit(solution)/shard_map/ppermute | solution.py:53
  31.9 0.0 collective-permute-done.5.refs_3_
  31.9 0.0 collective-permute-start.20
  31.9 5.0 %collective-permute-done.15.refs_5_ = bf16[256,512]{1,0:T(8,128)(2,1)S(1)} collective-permute-done((bf16[256,512]{1,0:T(8,128)(2,1)S(1)}, bf16[256,512]{1,0:T(8,128)(2,1)S(1)}, u32[]{:S(2)}, u32[]{:S(2)}) %collective-permute-start.15) | collective-permute-done | bytes 262176 | tf_op jit(solution)/shard_map/ppermute | solution.py:53
  36.9 0.0 collective-permute-start.21
  36.9 0.0 collective-permute-done.19.refs_2_
  36.9 1.6 %collective-permute-start.16 = (bf16[96,512]{1,0:T(8,128)(2,1)S(1)}, bf16[96,512]{1,0:T(8,128)(2,1)S(1)}, u32[]{:S(2)}, u32[]{:S(2)}) collective-permute-start(bf16[96,512]{1,0:T(8,128)(2,1)S(1)} %slice.9), channel_id=1, source_target_pairs={{0,2},{2,0},{4,6},{6,4},{1,3},{3,1},{5,7},{7,5},{8,10},{10,8},{12,... | collective-permute-start | bytes 294920 | tf_op jit(solution)/shard_map/ppermute | solution.py:53
  38.4 1.6 %fetch.1 = (bf16[128,4096]{1,0:T(8,128)(2,1)S(1)}, bf16[128,4096]{1,0:T(8,128)(2,1)S(1)}) custom-call(bf16[128,4096]{1,0:T(8,128)(2,1)} %bitcast.8, bf16[128,4096]{1,0:T(8,128)(2,1)} %bitcast.9), custom_call_target="tpu_custom_call" | custom-call | tf_op jit(solution)/shard_map/fetch/pallas_call | solution.py:132
  40.0 3.0 %attend.1 = (bf16[128,4096]{1,0:T(8,128)(2,1)S(1)}, f32[128,128]{1,0:T(8,128)S(1)}, bf16[128,2048]{1,0:T(8,128)(2,1)S(1)}, bf16[128,2048]{1,0:T(8,128)(2,1)S(1)}) custom-call(s32[1,8]{1,0:T(1,128)} %bitcast.15, bf16[128,4096]{1,0:T(8,128)(2,1)S(1)} %get-tuple-element.12.query_ref, bf16[128,4096]{1,0:T(8,128)(2,1)S(1)} %get-tuple-element.13.residual_ref, ...), custom_call_target="tpu_custom_call" | custom-call | tf_op jit(solution)/shard_map/attend/pallas_call | solution.py:259
  43.1 0.0 collective-permute-done.10.refs_8_
  43.1 1.6 %collective-permute-start.3 = (bf16[128,2048]{1,0:T(8,128)(2,1)S(1)}, bf16[128,2048]{1,0:T(8,128)(2,1)S(1)}, u32[]{:S(2)}, u32[]{:S(2)}) collective-permute-start(bf16[128,2048]{1,0:T(8,128)(2,1)S(1)} %get-tuple-element.17), channel_id=1, source_target_pairs={{0,8},{1,9},{8,0},{9,1},{16,24},{17,25},{24,16},{25,17},{2,10},{3,... | collective-permute-start | bytes 1572872 | tf_op jit(solution)/shard_map/ppermute | solution.py:49
  44.7 0.0 collective-permute-done.16.refs_2_
  44.7 0.0 collective-permute-start.18
  44.7 0.0 collective-permute-done.14.refs_1_
  44.7 0.5 collective-permute-start.4
  45.2 0.8 %collective-permute-done.18.refs_4_ = bf16[96,512]{1,0:T(8,128)(2,1)S(1)} collective-permute-done((bf16[96,512]{1,0:T(8,128)(2,1)S(1)}, bf16[96,512]{1,0:T(8,128)(2,1)S(1)}, u32[]{:S(2)}, u32[]{:S(2)}) %collective-permute-start.18) | collective-permute-done | bytes 98336 | tf_op jit(solution)/shard_map/ppermute | solution.py:53
  46.0 0.2 collective-permute-start.17
  46.2 0.0 collective-permute-done.20.refs_4_
  46.2 0.4 collective-permute-start.9
  46.5 0.0 collective-permute-done.21.refs_6_
  46.5 0.2 collective-permute-start.7
  46.7 0.7 %collective-permute-done.17.refs_3_ = bf16[160,512]{1,0:T(8,128)(2,1)S(1)} collective-permute-done((bf16[160,512]{1,0:T(8,128)(2,1)S(1)}, bf16[160,512]{1,0:T(8,128)(2,1)S(1)}, u32[]{:S(2)}, u32[]{:S(2)}) %collective-permute-start.17) | collective-permute-done | bytes 163872 | tf_op jit(solution)/shard_map/ppermute | solution.py:53
  47.4 0.2 collective-permute-start.11
  47.6 0.4 project.4.refs_5_
  48.0 0.2 project.5
  48.2 0.0 collective-permute-done.9.refs_7_
  48.2 0.6 %collective-permute-start.22 = (bf16[128,512]{1,0:T(8,128)(2,1)S(1)}, bf16[128,512]{1,0:T(8,128)(2,1)S(1)}, u32[]{:S(2)}, u32[]{:S(2)}) collective-permute-start(bf16[128,512]{1,0:T(8,128)(2,1)S(1)} %project.5), channel_id=1, source_target_pairs={{0,8},{1,9},{8,0},{9,1},{16,24},{17,25},{24,16},{25,17},{2,10},{3,... | collective-permute-start | bytes 393224 | tf_op jit(solution)/shard_map/ppermute | solution.py:49
  48.9 0.0 collective-permute-done.7.refs_5_
  48.9 0.1 collective-permute-start.23
  48.9 1.0 %store.1 = bf16[128,4096]{1,0:T(8,128)(2,1)} custom-call(bf16[128,4096]{1,0:T(8,128)(2,1)S(1)} %get-tuple-element.16.near_ref), custom_call_target="tpu_custom_call" | custom-call | tf_op jit(solution)/shard_map/store/pallas_call | solution.py:148
  49.9 8.0 %collective-permute-done.3.refs_0_ = bf16[128,2048]{1,0:T(8,128)(2,1)S(1)} collective-permute-done((bf16[128,2048]{1,0:T(8,128)(2,1)S(1)}, bf16[128,2048]{1,0:T(8,128)(2,1)S(1)}, u32[]{:S(2)}, u32[]{:S(2)}) %collective-permute-start.3) | collective-permute-done | bytes 524320 | tf_op jit(solution)/shard_map/ppermute | solution.py:49
  57.9 0.0 collective-permute-done.4.refs_1_
  57.9 0.0 collective-permute-done.11.refs_9_
  57.9 0.5 project.3.total_ref
  58.4 1.6 %collective-permute-done.22.refs_0_ = bf16[128,512]{1,0:T(8,128)(2,1)S(1)} collective-permute-done((bf16[128,512]{1,0:T(8,128)(2,1)S(1)}, bf16[128,512]{1,0:T(8,128)(2,1)S(1)}, u32[]{:S(2)}, u32[]{:S(2)}) %collective-permute-start.22) | collective-permute-done | bytes 131104 | tf_op jit(solution)/shard_map/ppermute | solution.py:49
  60.0 0.0 collective-permute-done.23.refs_1_
  60.0 0.7 %finish.1 = bf16[128,512]{1,0:T(8,128)(2,1)} custom-call(f32[128,512]{1,0:T(8,128)S(1)} %project.3.total_ref, bf16[128,512]{1,0:T(8,128)(2,1)S(1)} %collective-permute-done.22.refs_0_, bf16[128,512]{1,0:T(8,128)(2,1)S(1)} %collective-permute-done.23.refs_1_), custom_call_target="tpu_custom_call" | custom-call | tf_op jit(solution)/shard_map/finish/pallas_call | solution.py:336
  (2 shorter events, 0.0 us)
Async XLA Ops:
  1.9 11.3 %collective-permute-start.12 = (bf16[256,512]{1,0:T(8,128)(2,1)S(1)}, bf16[256,512]{1,0:T(8,128)(2,1)S(1)}, u32[]{:S(2)}, u32[]{:S(2)}) collective-permute-start(bf16[256,512]{1,0:T(8,128)(2,1)S(1)} %get-tuple-element.20), channel_id=1, source_target_pairs={{8,0},{16,8},{24,16},{9,1},{17,9},{25,17},{10,2},{18,10},{26,18},{... | collective-permute-start | bytes 786440 | tf_op jit(solution)/shard_map/ppermute | solution.py:38
  3.2 24.8 %collective-permute-start.8 = (bf16[256,512]{1,0:T(8,128)(2,1)S(1)}, bf16[256,512]{1,0:T(8,128)(2,1)S(1)}, u32[]{:S(2)}, u32[]{:S(2)}) collective-permute-start(bf16[256,512]{1,0:T(8,128)(2,1)S(1)} %get-tuple-element.18.refs_2_), channel_id=1, source_target_pairs={{0,4},{2,6},{4,0},{6,2},{1,5},{3,7},{5,1},{7,3},{8,12},{10,14},{12... | collective-permute-start | bytes 786440 | tf_op jit(solution)/shard_map/ppermute | solution.py:53
  13.2 15.1 %collective-permute-start.13 = (bf16[256,512]{1,0:T(8,128)(2,1)S(1)}, bf16[256,512]{1,0:T(8,128)(2,1)S(1)}, u32[]{:S(2)}, u32[]{:S(2)}) collective-permute-start(bf16[256,512]{1,0:T(8,128)(2,1)S(1)} %collective-permute-done.12.refs_1_), channel_id=1, source_target_pairs={{0,2},{2,0},{4,6},{6,4},{1,3},{3,1},{5,7},{7,5},{8,10},{10,8},{12,... | collective-permute-start | bytes 786440 | tf_op jit(solution)/shard_map/ppermute | solution.py:53
  14.8 12.9 %collective-permute-start = (bf16[128,512]{1,0:T(8,128)(2,1)S(1)}, bf16[128,512]{1,0:T(8,128)(2,1)S(1)}, u32[]{:S(2)}, u32[]{:S(2)}) collective-permute-start(bf16[128,512]{1,0:T(8,128)(2,1)S(1)} %get-tuple-element.14.refs_0_), channel_id=1, source_target_pairs={{0,2},{2,0},{4,6},{6,4},{1,3},{3,1},{5,7},{7,5},{8,10},{10,8},{12,... | collective-permute-start | bytes 393224 | tf_op jit(solution)/shard_map/ppermute | solution.py:53
  15.2 4.3 %collective-permute-start.1 = (bf16[64,512]{1,0:T(8,128)(2,1)S(1)}, bf16[64,512]{1,0:T(8,128)(2,1)S(1)}, u32[]{:S(2)}, u32[]{:S(2)}) collective-permute-start(bf16[64,512]{1,0:T(8,128)(2,1)S(1)} %get-tuple-element.15), channel_id=1, source_target_pairs={{0,4},{2,6},{4,0},{6,2},{1,5},{3,7},{5,1},{7,3},{8,12},{10,14},{12... | collective-permute-start | bytes 196616 | tf_op jit(solution)/shard_map/ppermute | solution.py:53
  16.9 10.8 %collective-permute-start.2 = (bf16[64,512]{1,0:T(8,128)(2,1)S(1)}, bf16[64,512]{1,0:T(8,128)(2,1)S(1)}, u32[]{:S(2)}, u32[]{:S(2)}) collective-permute-start(bf16[64,512]{1,0:T(8,128)(2,1)S(1)} %get-tuple-element.15), channel_id=1, source_target_pairs={{0,6},{2,4},{4,2},{6,0},{1,7},{3,5},{5,3},{7,1},{8,14},{10,12},{12... | collective-permute-start | bytes 196616 | tf_op jit(solution)/shard_map/ppermute | solution.py:53
  19.5 11.0 %collective-permute-start.6 = (bf16[256,512]{1,0:T(8,128)(2,1)S(1)}, bf16[256,512]{1,0:T(8,128)(2,1)S(1)}, u32[]{:S(2)}, u32[]{:S(2)}) collective-permute-start(bf16[256,512]{1,0:T(8,128)(2,1)S(1)} %get-tuple-element.18.refs_2_), channel_id=1, source_target_pairs={{0,2},{2,0},{4,6},{6,4},{1,3},{3,1},{5,7},{7,5},{8,10},{10,8},{12,... | collective-permute-start | bytes 786440 | tf_op jit(solution)/shard_map/ppermute | solution.py:53
  27.7 4.2 %collective-permute-start.5 = (bf16[256,512]{1,0:T(8,128)(2,1)S(1)}, bf16[256,512]{1,0:T(8,128)(2,1)S(1)}, u32[]{:S(2)}, u32[]{:S(2)}) collective-permute-start(bf16[256,512]{1,0:T(8,128)(2,1)S(1)} %get-tuple-element.18.refs_2_), channel_id=1, source_target_pairs={{0,1},{1,0},{2,3},{3,2},{4,5},{5,4},{6,7},{7,6},{8,9},{9,8},{10,11... | collective-permute-start | bytes 786440 | tf_op jit(solution)/shard_map/ppermute | solution.py:53
  27.7 9.2 %collective-permute-start.15 = (bf16[256,512]{1,0:T(8,128)(2,1)S(1)}, bf16[256,512]{1,0:T(8,128)(2,1)S(1)}, u32[]{:S(2)}, u32[]{:S(2)}) collective-permute-start(bf16[256,512]{1,0:T(8,128)(2,1)S(1)} %collective-permute-done.12.refs_1_), channel_id=1, source_target_pairs={{0,4},{2,6},{4,0},{6,2},{1,5},{3,7},{5,1},{7,3},{8,12},{10,14},{12... | collective-permute-start | bytes 786440 | tf_op jit(solution)/shard_map/ppermute | solution.py:53
  28.0 8.8 %collective-permute-start.19 = (bf16[256,512]{1,0:T(8,128)(2,1)S(1)}, bf16[256,512]{1,0:T(8,128)(2,1)S(1)}, u32[]{:S(2)}, u32[]{:S(2)}) collective-permute-start(bf16[256,512]{1,0:T(8,128)(2,1)S(1)} %collective-permute-done.12.refs_1_), channel_id=1, source_target_pairs={{0,1},{1,0},{2,3},{3,2},{4,5},{5,4},{6,7},{7,6},{8,9},{9,8},{10,11... | collective-permute-start | bytes 786440 | tf_op jit(solution)/shard_map/ppermute | solution.py:53
  28.3 14.8 %collective-permute-start.10 = (bf16[256,512]{1,0:T(8,128)(2,1)S(1)}, bf16[256,512]{1,0:T(8,128)(2,1)S(1)}, u32[]{:S(2)}, u32[]{:S(2)}) collective-permute-start(bf16[256,512]{1,0:T(8,128)(2,1)S(1)} %collective-permute-done.8.refs_6_), channel_id=1, source_target_pairs={{0,2},{2,0},{4,6},{6,4},{1,3},{3,1},{5,7},{7,5},{8,10},{10,8},{12,... | collective-permute-start | bytes 786440 | tf_op jit(solution)/shard_map/ppermute | solution.py:53
  30.5 14.2 %collective-permute-start.14 = (bf16[160,512]{1,0:T(8,128)(2,1)S(1)}, bf16[160,512]{1,0:T(8,128)(2,1)S(1)}, u32[]{:S(2)}, u32[]{:S(2)}) collective-permute-start(bf16[160,512]{1,0:T(8,128)(2,1)S(1)} %slice.8), channel_id=1, source_target_pairs={{0,4},{2,6},{4,0},{6,2},{1,5},{3,7},{5,1},{7,3},{8,12},{10,14},{12... | collective-permute-start | bytes 491528 | tf_op jit(solution)/shard_map/ppermute | solution.py:53
  31.9 14.3 %collective-permute-start.20 = (bf16[256,512]{1,0:T(8,128)(2,1)S(1)}, bf16[256,512]{1,0:T(8,128)(2,1)S(1)}, u32[]{:S(2)}, u32[]{:S(2)}) collective-permute-start(bf16[256,512]{1,0:T(8,128)(2,1)S(1)} %collective-permute-done.13.refs_3_), channel_id=1, source_target_pairs={{0,1},{1,0},{2,3},{3,2},{4,5},{5,4},{6,7},{7,6},{8,9},{9,8},{10,11... | collective-permute-start | bytes 786440 | tf_op jit(solution)/shard_map/ppermute | solution.py:53
  36.9 9.7 %collective-permute-start.21 = (bf16[256,512]{1,0:T(8,128)(2,1)S(1)}, bf16[256,512]{1,0:T(8,128)(2,1)S(1)}, u32[]{:S(2)}, u32[]{:S(2)}) collective-permute-start(bf16[256,512]{1,0:T(8,128)(2,1)S(1)} %collective-permute-done.15.refs_5_), channel_id=1, source_target_pairs={{0,1},{1,0},{2,3},{3,2},{4,5},{5,4},{6,7},{7,6},{8,9},{9,8},{10,11... | collective-permute-start | bytes 786440 | tf_op jit(solution)/shard_map/ppermute | solution.py:53
  36.9 7.8 %collective-permute-start.16 = (bf16[96,512]{1,0:T(8,128)(2,1)S(1)}, bf16[96,512]{1,0:T(8,128)(2,1)S(1)}, u32[]{:S(2)}, u32[]{:S(2)}) collective-permute-start(bf16[96,512]{1,0:T(8,128)(2,1)S(1)} %slice.9), channel_id=1, source_target_pairs={{0,2},{2,0},{4,6},{6,4},{1,3},{3,1},{5,7},{7,5},{8,10},{10,8},{12,... | collective-permute-start | bytes 294920 | tf_op jit(solution)/shard_map/ppermute | solution.py:53
  43.1 14.9 %collective-permute-start.3 = (bf16[128,2048]{1,0:T(8,128)(2,1)S(1)}, bf16[128,2048]{1,0:T(8,128)(2,1)S(1)}, u32[]{:S(2)}, u32[]{:S(2)}) collective-permute-start(bf16[128,2048]{1,0:T(8,128)(2,1)S(1)} %get-tuple-element.17), channel_id=1, source_target_pairs={{0,8},{1,9},{8,0},{9,1},{16,24},{17,25},{24,16},{25,17},{2,10},{3,... | collective-permute-start | bytes 1572872 | tf_op jit(solution)/shard_map/ppermute | solution.py:49
  44.7 1.3 %collective-permute-start.18 = (bf16[96,512]{1,0:T(8,128)(2,1)S(1)}, bf16[96,512]{1,0:T(8,128)(2,1)S(1)}, u32[]{:S(2)}, u32[]{:S(2)}) collective-permute-start(bf16[96,512]{1,0:T(8,128)(2,1)S(1)} %collective-permute-done.16.refs_2_), channel_id=1, source_target_pairs={{0,1},{1,0},{2,3},{3,2},{4,5},{5,4},{6,7},{7,6},{8,9},{9,8},{10,11... | collective-permute-start | bytes 294920 | tf_op jit(solution)/shard_map/ppermute | solution.py:53
  44.7 13.2 %collective-permute-start.4 = (bf16[128,2048]{1,0:T(8,128)(2,1)S(1)}, bf16[128,2048]{1,0:T(8,128)(2,1)S(1)}, u32[]{:S(2)}, u32[]{:S(2)}) collective-permute-start(bf16[128,2048]{1,0:T(8,128)(2,1)S(1)} %get-tuple-element.17), channel_id=1, source_target_pairs={{0,1},{1,0},{8,16},{9,17},{16,8},{17,9},{24,25},{25,24},{2,3},{3,2... | collective-permute-start | bytes 1572872 | tf_op jit(solution)/shard_map/ppermute | solution.py:49
  46.0 1.4 %collective-permute-start.17 = (bf16[160,512]{1,0:T(8,128)(2,1)S(1)}, bf16[160,512]{1,0:T(8,128)(2,1)S(1)}, u32[]{:S(2)}, u32[]{:S(2)}) collective-permute-start(bf16[160,512]{1,0:T(8,128)(2,1)S(1)} %collective-permute-done.14.refs_1_), channel_id=1, source_target_pairs={{0,1},{1,0},{2,3},{3,2},{4,5},{5,4},{6,7},{7,6},{8,9},{9,8},{10,11... | collective-permute-start | bytes 491528 | tf_op jit(solution)/shard_map/ppermute | solution.py:53
  46.2 2.0 %collective-permute-start.9 = (bf16[256,512]{1,0:T(8,128)(2,1)S(1)}, bf16[256,512]{1,0:T(8,128)(2,1)S(1)}, u32[]{:S(2)}, u32[]{:S(2)}) collective-permute-start(bf16[256,512]{1,0:T(8,128)(2,1)S(1)} %collective-permute-done.8.refs_6_), channel_id=1, source_target_pairs={{0,1},{1,0},{2,3},{3,2},{4,5},{5,4},{6,7},{7,6},{8,9},{9,8},{10,11... | collective-permute-start | bytes 786440 | tf_op jit(solution)/shard_map/ppermute | solution.py:53
  46.5 2.3 %collective-permute-start.7 = (bf16[256,512]{1,0:T(8,128)(2,1)S(1)}, bf16[256,512]{1,0:T(8,128)(2,1)S(1)}, u32[]{:S(2)}, u32[]{:S(2)}) collective-permute-start(bf16[256,512]{1,0:T(8,128)(2,1)S(1)} %collective-permute-done.6.refs_4_), channel_id=1, source_target_pairs={{0,1},{1,0},{2,3},{3,2},{4,5},{5,4},{6,7},{7,6},{8,9},{9,8},{10,11... | collective-permute-start | bytes 786440 | tf_op jit(solution)/shard_map/ppermute | solution.py:53
  47.4 10.5 %collective-permute-start.11 = (bf16[256,512]{1,0:T(8,128)(2,1)S(1)}, bf16[256,512]{1,0:T(8,128)(2,1)S(1)}, u32[]{:S(2)}, u32[]{:S(2)}) collective-permute-start(bf16[256,512]{1,0:T(8,128)(2,1)S(1)} %collective-permute-done.10.refs_8_), channel_id=1, source_target_pairs={{0,1},{1,0},{2,3},{3,2},{4,5},{5,4},{6,7},{7,6},{8,9},{9,8},{10,11... | collective-permute-start | bytes 786440 | tf_op jit(solution)/shard_map/ppermute | solution.py:53
  48.2 11.8 %collective-permute-start.22 = (bf16[128,512]{1,0:T(8,128)(2,1)S(1)}, bf16[128,512]{1,0:T(8,128)(2,1)S(1)}, u32[]{:S(2)}, u32[]{:S(2)}) collective-permute-start(bf16[128,512]{1,0:T(8,128)(2,1)S(1)} %project.5), channel_id=1, source_target_pairs={{0,8},{1,9},{8,0},{9,1},{16,24},{17,25},{24,16},{25,17},{2,10},{3,... | collective-permute-start | bytes 393224 | tf_op jit(solution)/shard_map/ppermute | solution.py:49
  48.9 11.1 %collective-permute-start.23 = (bf16[128,512]{1,0:T(8,128)(2,1)S(1)}, bf16[128,512]{1,0:T(8,128)(2,1)S(1)}, u32[]{:S(2)}, u32[]{:S(2)}) collective-permute-start(bf16[128,512]{1,0:T(8,128)(2,1)S(1)} %project.5), channel_id=1, source_target_pairs={{0,1},{1,0},{8,16},{9,17},{16,8},{17,9},{24,25},{25,24},{2,3},{3,2... | collective-permute-start | bytes 393224 | tf_op jit(solution)/shard_map/ppermute | solution.py:49

commit v3 on v2

--- a/solution.py
+++ b/solution.py
@@ -14,7 +14,7 @@
 
 epsilon = 1e-06
 MASKED = -1e30
-FEWER = 96
+FEWER = 112
 
 WHOLE = pl.BlockSpec(memory_space=pltpu.VMEM)
 FAR = pl.BlockSpec(memory_space=pltpu.HBM)
@@ -71,16 +71,20 @@
     width = key_ref.shape[1]
     depth = weight_ref.shape[0]
     at = (lax.axis_index("seq") * lax.axis_size("exp") + lax.axis_index("exp")) * depth
-    run_copies(
+    loads = [pltpu.make_async_copy(gain_ref, gain, sems.at[1]), pltpu.make_async_copy(weight_ref, weight, sems.at[0])]
+    for load in loads:
+        load.start()
+    rest = (
         [
-            pltpu.make_async_copy(weight_ref, weight, sems.at[0]),
-            pltpu.make_async_copy(gain_ref, gain, sems.at[1]),
             pltpu.make_async_copy(key_ref, pair_ref.at[:, :width], sems.at[2]),
             pltpu.make_async_copy(value_ref, pair_ref.at[:, width:], sems.at[3]),
             pltpu.make_async_copy(key_ref.at[sent], half_ref.at[:, :width], sems.at[4]),
             pltpu.make_async_copy(value_ref.at[sent], half_ref.at[:, width:], sems.at[5]),
         ]
     )
+    for copy in rest:
+        copy.start()
+    loads[0].wait()
     if depth % DH:
         wide = gain[...]
         place = lax.broadcasted_iota(jnp.int32, (depth, wide.shape[1]), 0) + at
@@ -89,12 +93,15 @@
     else:
         wide = gain[:, pl.ds(pl.multiple_of(at, depth), depth)]
         column = jnp.transpose(jnp.broadcast_to(wide, (DH, depth)))
+    loads[1].wait()
     rows = depth // len(piece_refs)
     for index, piece_ref in enumerate(piece_refs):
         part = slice(index * rows, (index + 1) * rows)
         for left in range(0, weight.shape[1], DH):
             cols = slice(left, left + DH)
             piece_ref[:, cols] = (weight[part, cols].astype(jnp.float32) * column[part]).astype(jnp.bfloat16)
+    for copy in rest:
+        copy.wait()
 
 
 def prepare(key_rows, value_rows, norm_gain, weight, pieces):
@@ -368,8 +375,8 @@
     pair, half, leaves, stays = prepare(key_rows, value_rows, norm_gain, weight, 2)
     leaves = shifted(leaves, -1)
     rows = leaves.shape[0]
-    leaves_early, leaves_late = gather_square(leaves, ((1, rows - FEWER), (2, FEWER)))
-    stays_early, stays_late = gather_square(stays, ((2, rows),))
+    leaves_early, leaves_late = gather_square(leaves, ((2, rows - FEWER), (1, FEWER)))
+    stays_early, stays_late = gather_square(stays, ((1, rows),))
     pairs = [pair, exchanged(pair, "seq", 1)]
     pairs.append(exchanged(half, "seq", 2))
     pairs.append(exchanged(half, "seq", 3))

time: 60.9 us -> 57.4 us (0.943)
  waiting for transfers between devices: 31.3 us -> 25.8 us
  starting transfers between devices: 20 us -> 22 us
    ppermute x19, waiting for transfers between devices: 14.8 us -> 9.67 us  [exchanged(): lax.ppermute(block, axis, [(i, i ^ bit) for i in range(lax.axis_size(axis...]
    ppermute x19, starting transfers between devices: 15.9 us -> 17.8 us  [exchanged(): lax.ppermute(block, axis, [(i, i ^ bit) for i in range(lax.axis_size(axis...]
  transfers between devices with their start and end apart: 24 -> 24, of which waited for: 9 -> 8; matrix products, arithmetic and copies ran while one was open for 0% -> 0% of each run, Pallas kernels for 11% -> 12%
where the time goes in v3:
time: 57.4 us; the launch traced here: 57.1 us
  waiting for transfers between devices  25.8 us (45%)
  starting transfers between devices  22 us (38%)
  Pallas kernels  8.61 us (15%)
  between operations  0.75 us (1%)
    ppermute x19, starting transfers between devices, exchanged(): lax.ppermute(block, axis, [(i, i ^ bit) for i in range(lax.axis_size(axis...  17.8 us
    ppermute x19, waiting for transfers between devices, exchanged(): lax.ppermute(block, axis, [(i, i ^ bit) for i in range(lax.axis_size(axis...  9.67 us
    ppermute x4, waiting for transfers between devices, paired(): return lax.ppermute(block, ('pipe', 'exp'), route)  9.2 us
    ppermute x1, waiting for transfers between devices, shifted(): return lax.ppermute(block, 'pipe', route)  6.93 us
    pallas_call x1, Pallas kernels, attend(): pl.pallas_call(functools.partial(attend_kernel, groups, longest, 1.0 / ma...  3.04 us
    ppermute x4, starting transfers between devices, paired(): return lax.ppermute(block, ('pipe', 'exp'), route)  2.84 us
    pallas_call x1, Pallas kernels, fetch(): pl.pallas_call(fetch_kernel, out_shape=tuple((pltpu.VMEM(array.shape, arr...  1.56 us
    ppermute x1, starting transfers between devices, shifted(): return lax.ppermute(block, 'pipe', route)  1.29 us
  transfers between devices with their start and end apart: 24, of which 8 were waited for; matrix products, arithmetic and copies ran while one was open for 0% of the time, Pallas kernels for 12%

profile of v3, /device:TPU:0, one launch (start us, length us, event | category | flops | bytes accessed | tf_op | source)
XLA Modules:
  0.0 57.1 jit_solution(5603592089155864268)
XLA Ops:
  0.6 1.2 %prepare.1 = (bf16[128,512]{1,0:T(8,128)(2,1)S(1)}, bf16[64,512]{1,0:T(8,128)(2,1)S(1)}, bf16[256,512]{1,0:T(8,128)(2,1)S(1)}, bf16[256,512]{1,0:T(8,128)(2,1)S(1)}) custom-call(bf16[128,256]{1,0:T(8,128)(2,1)} %bitcast.13, bf16[128,256]{1,0:T(8,128)(2,1)} %bitcast.14, f32[1,4096]{1,0:T(1,128)} %gain_ref.1, bf16[512,512]{1,0:T(8,128)(2,1)} %bitcast.11), custom_call_target="tpu_custom_call" | custom-call | tf_op jit(solution)/shard_map/prepare/pallas_call | solution.py:111
  1.9 1.3 %collective-permute-start.12 = (bf16[256,512]{1,0:T(8,128)(2,1)S(1)}, bf16[256,512]{1,0:T(8,128)(2,1)S(1)}, u32[]{:S(2)}, u32[]{:S(2)}) collective-permute-start(bf16[256,512]{1,0:T(8,128)(2,1)S(1)} %get-tuple-element.20), channel_id=1, source_target_pairs={{8,0},{16,8},{24,16},{9,1},{17,9},{25,17},{10,2},{18,10},{26,18},{... | collective-permute-start | bytes 786440 | tf_op jit(solution)/shard_map/ppermute | solution.py:38
  3.2 3.0 %collective-permute-start.6 = (bf16[256,512]{1,0:T(8,128)(2,1)S(1)}, bf16[256,512]{1,0:T(8,128)(2,1)S(1)}, u32[]{:S(2)}, u32[]{:S(2)}) collective-permute-start(bf16[256,512]{1,0:T(8,128)(2,1)S(1)} %get-tuple-element.18.refs_2_), channel_id=1, source_target_pairs={{0,2},{2,0},{4,6},{6,4},{1,3},{3,1},{5,7},{7,5},{8,10},{10,8},{12,... | collective-permute-start | bytes 786440 | tf_op jit(solution)/shard_map/ppermute | solution.py:53
  6.2 6.9 %collective-permute-done.12.refs_1_ = bf16[256,512]{1,0:T(8,128)(2,1)S(1)} collective-permute-done((bf16[256,512]{1,0:T(8,128)(2,1)S(1)}, bf16[256,512]{1,0:T(8,128)(2,1)S(1)}, u32[]{:S(2)}, u32[]{:S(2)}) %collective-permute-start.12) | collective-permute-done | bytes 262176 | tf_op jit(solution)/shard_map/ppermute | solution.py:38
  13.1 1.7 %collective-permute-start.13 = (bf16[256,512]{1,0:T(8,128)(2,1)S(1)}, bf16[256,512]{1,0:T(8,128)(2,1)S(1)}, u32[]{:S(2)}, u32[]{:S(2)}) collective-permute-start(bf16[256,512]{1,0:T(8,128)(2,1)S(1)} %collective-permute-done.12.refs_1_), channel_id=1, source_target_pairs={{0,4},{2,6},{4,0},{6,2},{1,5},{3,7},{5,1},{7,3},{8,12},{10,14},{12... | collective-permute-start | bytes 786440 | tf_op jit(solution)/shard_map/ppermute | solution.py:53
  14.8 1.5 %collective-permute-start = (bf16[128,512]{1,0:T(8,128)(2,1)S(1)}, bf16[128,512]{1,0:T(8,128)(2,1)S(1)}, u32[]{:S(2)}, u32[]{:S(2)}) collective-permute-start(bf16[128,512]{1,0:T(8,128)(2,1)S(1)} %get-tuple-element.14.refs_0_), channel_id=1, source_target_pairs={{0,2},{2,0},{4,6},{6,4},{1,3},{3,1},{5,7},{7,5},{8,10},{10,8},{12,... | collective-permute-start | bytes 393224 | tf_op jit(solution)/shard_map/ppermute | solution.py:53
  16.3 0.5 collective-permute-start.1
  16.8 1.5 %collective-permute-start.2 = (bf16[64,512]{1,0:T(8,128)(2,1)S(1)}, bf16[64,512]{1,0:T(8,128)(2,1)S(1)}, u32[]{:S(2)}, u32[]{:S(2)}) collective-permute-start(bf16[64,512]{1,0:T(8,128)(2,1)S(1)} %get-tuple-element.15), channel_id=1, source_target_pairs={{0,6},{2,4},{4,2},{6,0},{1,7},{3,5},{5,3},{7,1},{8,14},{10,12},{12... | collective-permute-start | bytes 196616 | tf_op jit(solution)/shard_map/ppermute | solution.py:53
  18.3 5.1 %collective-permute-done.1.refs_2_ = bf16[64,512]{1,0:T(8,128)(2,1)S(1)} collective-permute-done((bf16[64,512]{1,0:T(8,128)(2,1)S(1)}, bf16[64,512]{1,0:T(8,128)(2,1)S(1)}, u32[]{:S(2)}, u32[]{:S(2)}) %collective-permute-start.1) | collective-permute-done | bytes 65568 | tf_op jit(solution)/shard_map/ppermute | solution.py:53
  23.4 1.4 %collective-permute-start.8 = (bf16[256,512]{1,0:T(8,128)(2,1)S(1)}, bf16[256,512]{1,0:T(8,128)(2,1)S(1)}, u32[]{:S(2)}, u32[]{:S(2)}) collective-permute-start(bf16[256,512]{1,0:T(8,128)(2,1)S(1)} %get-tuple-element.18.refs_2_), channel_id=1, source_target_pairs={{0,4},{2,6},{4,0},{6,2},{1,5},{3,7},{5,1},{7,3},{8,12},{10,14},{12... | collective-permute-start | bytes 786440 | tf_op jit(solution)/shard_map/ppermute | solution.py:53
  24.8 0.0 collective-permute-done.2.refs_3_
  24.8 1.5 %collective-permute-start.15 = (bf16[256,512]{1,0:T(8,128)(2,1)S(1)}, bf16[256,512]{1,0:T(8,128)(2,1)S(1)}, u32[]{:S(2)}, u32[]{:S(2)}) collective-permute-start(bf16[256,512]{1,0:T(8,128)(2,1)S(1)} %collective-permute-done.12.refs_1_), channel_id=1, source_target_pairs={{0,2},{2,0},{4,6},{6,4},{1,3},{3,1},{5,7},{7,5},{8,10},{10,8},{12,... | collective-permute-start | bytes 786440 | tf_op jit(solution)/shard_map/ppermute | solution.py:53
  26.3 0.0 collective-permute-done.refs_1_
  26.3 0.0 collective-permute-start.5
  26.3 0.0 collective-permute-done.6.refs_4_
  26.3 0.5 collective-permute-start.19
  26.8 0.0 collective-permute-done.13.refs_5_
  26.8 0.5 collective-permute-start.10
  27.3 2.7 %collective-permute-done.8.refs_6_ = bf16[256,512]{1,0:T(8,128)(2,1)S(1)} collective-permute-done((bf16[256,512]{1,0:T(8,128)(2,1)S(1)}, bf16[256,512]{1,0:T(8,128)(2,1)S(1)}, u32[]{:S(2)}, u32[]{:S(2)}) %collective-permute-start.8) | collective-permute-done | bytes 262176 | tf_op jit(solution)/shard_map/ppermute | solution.py:53
  30.1 2.2 %collective-permute-start.14 = (bf16[144,512]{1,0:T(8,128)(2,1)S(1)}, bf16[144,512]{1,0:T(8,128)(2,1)S(1)}, u32[]{:S(2)}, u32[]{:S(2)}) collective-permute-start(bf16[144,512]{1,0:T(8,128)(2,1)S(1)} %slice.8), channel_id=1, source_target_pairs={{0,2},{2,0},{4,6},{6,4},{1,3},{3,1},{5,7},{7,5},{8,10},{10,8},{12,... | collective-permute-start | bytes 442376 | tf_op jit(solution)/shard_map/ppermute | solution.py:53
  32.3 0.3 collective-permute-done.15.refs_3_
  32.6 0.0 collective-permute-start.20
  32.6 0.0 collective-permute-done.5.refs_3_
  32.6 0.5 collective-permute-start.21
  33.1 0.0 collective-permute-done.19.refs_2_
  33.1 2.2 %collective-permute-start.16 = (bf16[112,512]{1,0:T(8,128)(2,1)S(1)}, bf16[112,512]{1,0:T(8,128)(2,1)S(1)}, u32[]{:S(2)}, u32[]{:S(2)}) collective-permute-start(bf16[112,512]{1,0:T(8,128)(2,1)S(1)} %slice.9), channel_id=1, source_target_pairs={{0,4},{2,6},{4,0},{6,2},{1,5},{3,7},{5,1},{7,3},{8,12},{10,14},{12... | collective-permute-start | bytes 344072 | tf_op jit(solution)/shard_map/ppermute | solution.py:53
  35.3 1.6 %fetch.1 = (bf16[128,4096]{1,0:T(8,128)(2,1)S(1)}, bf16[128,4096]{1,0:T(8,128)(2,1)S(1)}) custom-call(bf16[128,4096]{1,0:T(8,128)(2,1)} %bitcast.8, bf16[128,4096]{1,0:T(8,128)(2,1)} %bitcast.9), custom_call_target="tpu_custom_call" | custom-call | tf_op jit(solution)/shard_map/fetch/pallas_call | solution.py:139
  36.8 3.0 %attend.1 = (bf16[128,4096]{1,0:T(8,128)(2,1)S(1)}, f32[128,128]{1,0:T(8,128)S(1)}, bf16[128,2048]{1,0:T(8,128)(2,1)S(1)}, bf16[128,2048]{1,0:T(8,128)(2,1)S(1)}) custom-call(s32[1,8]{1,0:T(1,128)} %bitcast.15, bf16[128,4096]{1,0:T(8,128)(2,1)S(1)} %get-tuple-element.12.query_ref, bf16[128,4096]{1,0:T(8,128)(2,1)S(1)} %get-tuple-element.13.residual_ref, ...), custom_call_target="tpu_custom_call" | custom-call | tf_op jit(solution)/shard_map/attend/pallas_call | solution.py:266
  39.9 0.0 collective-permute-done.10.refs_8_
  39.9 1.8 %collective-permute-start.3 = (bf16[128,2048]{1,0:T(8,128)(2,1)S(1)}, bf16[128,2048]{1,0:T(8,128)(2,1)S(1)}, u32[]{:S(2)}, u32[]{:S(2)}) collective-permute-start(bf16[128,2048]{1,0:T(8,128)(2,1)S(1)} %get-tuple-element.17), channel_id=1, source_target_pairs={{0,8},{1,9},{8,0},{9,1},{16,24},{17,25},{24,16},{25,17},{2,10},{3,... | collective-permute-start | bytes 1572872 | tf_op jit(solution)/shard_map/ppermute | solution.py:49
  41.7 0.0 collective-permute-done.16.refs_2_
  41.7 0.0 collective-permute-start.18
  41.7 0.0 collective-permute-done.14.refs_1_
  41.7 0.5 collective-permute-start.4
  42.2 0.8 %collective-permute-done.18.refs_4_ = bf16[112,512]{1,0:T(8,128)(2,1)S(1)} collective-permute-done((bf16[112,512]{1,0:T(8,128)(2,1)S(1)}, bf16[112,512]{1,0:T(8,128)(2,1)S(1)}, u32[]{:S(2)}, u32[]{:S(2)}) %collective-permute-start.18) | collective-permute-done | bytes 114720 | tf_op jit(solution)/shard_map/ppermute | solution.py:53
  43.0 0.2 collective-permute-start.17
  43.2 0.0 collective-permute-done.20.refs_4_
  43.2 0.4 collective-permute-start.7
  43.5 0.0 collective-permute-done.21.refs_6_
  43.5 0.2 collective-permute-start.9
  43.7 0.7 %collective-permute-done.17.refs_3_ = bf16[144,512]{1,0:T(8,128)(2,1)S(1)} collective-permute-done((bf16[144,512]{1,0:T(8,128)(2,1)S(1)}, bf16[144,512]{1,0:T(8,128)(2,1)S(1)}, u32[]{:S(2)}, u32[]{:S(2)}) %collective-permute-start.17) | collective-permute-done | bytes 147488 | tf_op jit(solution)/shard_map/ppermute | solution.py:53
  44.4 0.2 collective-permute-start.11
  44.5 0.4 project.4.refs_5_
  44.9 0.2 project.5
  45.2 0.0 collective-permute-done.7.refs_5_
  45.2 0.5 collective-permute-start.22
  45.7 0.0 collective-permute-done.9.refs_7_
  45.7 0.1 collective-permute-start.23
  45.7 1.0 %store.1 = bf16[128,4096]{1,0:T(8,128)(2,1)} custom-call(bf16[128,4096]{1,0:T(8,128)(2,1)S(1)} %get-tuple-element.16.near_ref), custom_call_target="tpu_custom_call" | custom-call | tf_op jit(solution)/shard_map/store/pallas_call | solution.py:155
  46.7 8.0 %collective-permute-done.3.refs_0_ = bf16[128,2048]{1,0:T(8,128)(2,1)S(1)} collective-permute-done((bf16[128,2048]{1,0:T(8,128)(2,1)S(1)}, bf16[128,2048]{1,0:T(8,128)(2,1)S(1)}, u32[]{:S(2)}, u32[]{:S(2)}) %collective-permute-start.3) | collective-permute-done | bytes 524320 | tf_op jit(solution)/shard_map/ppermute | solution.py:49
  54.8 0.0 collective-permute-done.4.refs_1_
  54.8 0.0 collective-permute-done.11.refs_9_
  54.8 0.5 project.3.total_ref
  55.2 1.2 %collective-permute-done.22.refs_0_ = bf16[128,512]{1,0:T(8,128)(2,1)S(1)} collective-permute-done((bf16[128,512]{1,0:T(8,128)(2,1)S(1)}, bf16[128,512]{1,0:T(8,128)(2,1)S(1)}, u32[]{:S(2)}, u32[]{:S(2)}) %collective-permute-start.22) | collective-permute-done | bytes 131104 | tf_op jit(solution)/shard_map/ppermute | solution.py:49
  56.4 0.0 collective-permute-done.23.refs_1_
  56.4 0.7 %finish.1 = bf16[128,512]{1,0:T(8,128)(2,1)} custom-call(f32[128,512]{1,0:T(8,128)S(1)} %project.3.total_ref, bf16[128,512]{1,0:T(8,128)(2,1)S(1)} %collective-permute-done.22.refs_0_, bf16[128,512]{1,0:T(8,128)(2,1)S(1)} %collective-permute-done.23.refs_1_), custom_call_target="tpu_custom_call" | custom-call | tf_op jit(solution)/shard_map/finish/pallas_call | solution.py:343
  (2 shorter events, 0.0 us)
Async XLA Ops:
  1.9 11.3 %collective-permute-start.12 = (bf16[256,512]{1,0:T(8,128)(2,1)S(1)}, bf16[256,512]{1,0:T(8,128)(2,1)S(1)}, u32[]{:S(2)}, u32[]{:S(2)}) collective-permute-start(bf16[256,512]{1,0:T(8,128)(2,1)S(1)} %get-tuple-element.20), channel_id=1, source_target_pairs={{8,0},{16,8},{24,16},{9,1},{17,9},{25,17},{10,2},{18,10},{26,18},{... | collective-permute-start | bytes 786440 | tf_op jit(solution)/shard_map/ppermute | solution.py:38
  3.2 23.1 %collective-permute-start.6 = (bf16[256,512]{1,0:T(8,128)(2,1)S(1)}, bf16[256,512]{1,0:T(8,128)(2,1)S(1)}, u32[]{:S(2)}, u32[]{:S(2)}) collective-permute-start(bf16[256,512]{1,0:T(8,128)(2,1)S(1)} %get-tuple-element.18.refs_2_), channel_id=1, source_target_pairs={{0,2},{2,0},{4,6},{6,4},{1,3},{3,1},{5,7},{7,5},{8,10},{10,8},{12,... | collective-permute-start | bytes 786440 | tf_op jit(solution)/shard_map/ppermute | solution.py:53
  13.1 13.7 %collective-permute-start.13 = (bf16[256,512]{1,0:T(8,128)(2,1)S(1)}, bf16[256,512]{1,0:T(8,128)(2,1)S(1)}, u32[]{:S(2)}, u32[]{:S(2)}) collective-permute-start(bf16[256,512]{1,0:T(8,128)(2,1)S(1)} %collective-permute-done.12.refs_1_), channel_id=1, source_target_pairs={{0,4},{2,6},{4,0},{6,2},{1,5},{3,7},{5,1},{7,3},{8,12},{10,14},{12... | collective-permute-start | bytes 786440 | tf_op jit(solution)/shard_map/ppermute | solution.py:53
  14.8 11.5 %collective-permute-start = (bf16[128,512]{1,0:T(8,128)(2,1)S(1)}, bf16[128,512]{1,0:T(8,128)(2,1)S(1)}, u32[]{:S(2)}, u32[]{:S(2)}) collective-permute-start(bf16[128,512]{1,0:T(8,128)(2,1)S(1)} %get-tuple-element.14.refs_0_), channel_id=1, source_target_pairs={{0,2},{2,0},{4,6},{6,4},{1,3},{3,1},{5,7},{7,5},{8,10},{10,8},{12,... | collective-permute-start | bytes 393224 | tf_op jit(solution)/shard_map/ppermute | solution.py:53
  16.3 7.1 %collective-permute-start.1 = (bf16[64,512]{1,0:T(8,128)(2,1)S(1)}, bf16[64,512]{1,0:T(8,128)(2,1)S(1)}, u32[]{:S(2)}, u32[]{:S(2)}) collective-permute-start(bf16[64,512]{1,0:T(8,128)(2,1)S(1)} %get-tuple-element.15), channel_id=1, source_target_pairs={{0,4},{2,6},{4,0},{6,2},{1,5},{3,7},{5,1},{7,3},{8,12},{10,14},{12... | collective-permute-start | bytes 196616 | tf_op jit(solution)/shard_map/ppermute | solution.py:53
  16.8 8.0 %collective-permute-start.2 = (bf16[64,512]{1,0:T(8,128)(2,1)S(1)}, bf16[64,512]{1,0:T(8,128)(2,1)S(1)}, u32[]{:S(2)}, u32[]{:S(2)}) collective-permute-start(bf16[64,512]{1,0:T(8,128)(2,1)S(1)} %get-tuple-element.15), channel_id=1, source_target_pairs={{0,6},{2,4},{4,2},{6,0},{1,7},{3,5},{5,3},{7,1},{8,14},{10,12},{12... | collective-permute-start | bytes 196616 | tf_op jit(solution)/shard_map/ppermute | solution.py:53
  23.4 6.7 %collective-permute-start.8 = (bf16[256,512]{1,0:T(8,128)(2,1)S(1)}, bf16[256,512]{1,0:T(8,128)(2,1)S(1)}, u32[]{:S(2)}, u32[]{:S(2)}) collective-permute-start(bf16[256,512]{1,0:T(8,128)(2,1)S(1)} %get-tuple-element.18.refs_2_), channel_id=1, source_target_pairs={{0,4},{2,6},{4,0},{6,2},{1,5},{3,7},{5,1},{7,3},{8,12},{10,14},{12... | collective-permute-start | bytes 786440 | tf_op jit(solution)/shard_map/ppermute | solution.py:53
  24.8 7.8 %collective-permute-start.15 = (bf16[256,512]{1,0:T(8,128)(2,1)S(1)}, bf16[256,512]{1,0:T(8,128)(2,1)S(1)}, u32[]{:S(2)}, u32[]{:S(2)}) collective-permute-start(bf16[256,512]{1,0:T(8,128)(2,1)S(1)} %collective-permute-done.12.refs_1_), channel_id=1, source_target_pairs={{0,2},{2,0},{4,6},{6,4},{1,3},{3,1},{5,7},{7,5},{8,10},{10,8},{12,... | collective-permute-start | bytes 786440 | tf_op jit(solution)/shard_map/ppermute | solution.py:53
  26.3 6.3 %collective-permute-start.5 = (bf16[256,512]{1,0:T(8,128)(2,1)S(1)}, bf16[256,512]{1,0:T(8,128)(2,1)S(1)}, u32[]{:S(2)}, u32[]{:S(2)}) collective-permute-start(bf16[256,512]{1,0:T(8,128)(2,1)S(1)} %get-tuple-element.18.refs_2_), channel_id=1, source_target_pairs={{0,1},{1,0},{2,3},{3,2},{4,5},{5,4},{6,7},{7,6},{8,9},{9,8},{10,11... | collective-permute-start | bytes 786440 | tf_op jit(solution)/shard_map/ppermute | solution.py:53
  26.3 6.8 %collective-permute-start.19 = (bf16[256,512]{1,0:T(8,128)(2,1)S(1)}, bf16[256,512]{1,0:T(8,128)(2,1)S(1)}, u32[]{:S(2)}, u32[]{:S(2)}) collective-permute-start(bf16[256,512]{1,0:T(8,128)(2,1)S(1)} %collective-permute-done.12.refs_1_), channel_id=1, source_target_pairs={{0,1},{1,0},{2,3},{3,2},{4,5},{5,4},{6,7},{7,6},{8,9},{9,8},{10,11... | collective-permute-start | bytes 786440 | tf_op jit(solution)/shard_map/ppermute | solution.py:53
  26.8 13.1 %collective-permute-start.10 = (bf16[256,512]{1,0:T(8,128)(2,1)S(1)}, bf16[256,512]{1,0:T(8,128)(2,1)S(1)}, u32[]{:S(2)}, u32[]{:S(2)}) collective-permute-start(bf16[256,512]{1,0:T(8,128)(2,1)S(1)} %collective-permute-done.6.refs_4_), channel_id=1, source_target_pairs={{0,4},{2,6},{4,0},{6,2},{1,5},{3,7},{5,1},{7,3},{8,12},{10,14},{12... | collective-permute-start | bytes 786440 | tf_op jit(solution)/shard_map/ppermute | solution.py:53
  30.1 11.6 %collective-permute-start.14 = (bf16[144,512]{1,0:T(8,128)(2,1)S(1)}, bf16[144,512]{1,0:T(8,128)(2,1)S(1)}, u32[]{:S(2)}, u32[]{:S(2)}) collective-permute-start(bf16[144,512]{1,0:T(8,128)(2,1)S(1)} %slice.8), channel_id=1, source_target_pairs={{0,2},{2,0},{4,6},{6,4},{1,3},{3,1},{5,7},{7,5},{8,10},{10,8},{12,... | collective-permute-start | bytes 442376 | tf_op jit(solution)/shard_map/ppermute | solution.py:53
  32.6 10.6 %collective-permute-start.20 = (bf16[256,512]{1,0:T(8,128)(2,1)S(1)}, bf16[256,512]{1,0:T(8,128)(2,1)S(1)}, u32[]{:S(2)}, u32[]{:S(2)}) collective-permute-start(bf16[256,512]{1,0:T(8,128)(2,1)S(1)} %collective-permute-done.15.refs_3_), channel_id=1, source_target_pairs={{0,1},{1,0},{2,3},{3,2},{4,5},{5,4},{6,7},{7,6},{8,9},{9,8},{10,11... | collective-permute-start | bytes 786440 | tf_op jit(solution)/shard_map/ppermute | solution.py:53
  32.6 11.0 %collective-permute-start.21 = (bf16[256,512]{1,0:T(8,128)(2,1)S(1)}, bf16[256,512]{1,0:T(8,128)(2,1)S(1)}, u32[]{:S(2)}, u32[]{:S(2)}) collective-permute-start(bf16[256,512]{1,0:T(8,128)(2,1)S(1)} %collective-permute-done.13.refs_5_), channel_id=1, source_target_pairs={{0,1},{1,0},{2,3},{3,2},{4,5},{5,4},{6,7},{7,6},{8,9},{9,8},{10,11... | collective-permute-start | bytes 786440 | tf_op jit(solution)/shard_map/ppermute | solution.py:53
  33.1 8.6 %collective-permute-start.16 = (bf16[112,512]{1,0:T(8,128)(2,1)S(1)}, bf16[112,512]{1,0:T(8,128)(2,1)S(1)}, u32[]{:S(2)}, u32[]{:S(2)}) collective-permute-start(bf16[112,512]{1,0:T(8,128)(2,1)S(1)} %slice.9), channel_id=1, source_target_pairs={{0,4},{2,6},{4,0},{6,2},{1,5},{3,7},{5,1},{7,3},{8,12},{10,14},{12... | collective-permute-start | bytes 344072 | tf_op jit(solution)/shard_map/ppermute | solution.py:53
  39.9 14.9 %collective-permute-start.3 = (bf16[128,2048]{1,0:T(8,128)(2,1)S(1)}, bf16[128,2048]{1,0:T(8,128)(2,1)S(1)}, u32[]{:S(2)}, u32[]{:S(2)}) collective-permute-start(bf16[128,2048]{1,0:T(8,128)(2,1)S(1)} %get-tuple-element.17), channel_id=1, source_target_pairs={{0,8},{1,9},{8,0},{9,1},{16,24},{17,25},{24,16},{25,17},{2,10},{3,... | collective-permute-start | bytes 1572872 | tf_op jit(solution)/shard_map/ppermute | solution.py:49
  41.7 1.3 %collective-permute-start.18 = (bf16[112,512]{1,0:T(8,128)(2,1)S(1)}, bf16[112,512]{1,0:T(8,128)(2,1)S(1)}, u32[]{:S(2)}, u32[]{:S(2)}) collective-permute-start(bf16[112,512]{1,0:T(8,128)(2,1)S(1)} %collective-permute-done.16.refs_2_), channel_id=1, source_target_pairs={{0,1},{1,0},{2,3},{3,2},{4,5},{5,4},{6,7},{7,6},{8,9},{9,8},{10,11... | collective-permute-start | bytes 344072 | tf_op jit(solution)/shard_map/ppermute | solution.py:53
  41.7 13.1 %collective-permute-start.4 = (bf16[128,2048]{1,0:T(8,128)(2,1)S(1)}, bf16[128,2048]{1,0:T(8,128)(2,1)S(1)}, u32[]{:S(2)}, u32[]{:S(2)}) collective-permute-start(bf16[128,2048]{1,0:T(8,128)(2,1)S(1)} %get-tuple-element.17), channel_id=1, source_target_pairs={{0,1},{1,0},{8,16},{9,17},{16,8},{17,9},{24,25},{25,24},{2,3},{3,2... | collective-permute-start | bytes 1572872 | tf_op jit(solution)/shard_map/ppermute | solution.py:49
  43.0 1.4 %collective-permute-start.17 = (bf16[144,512]{1,0:T(8,128)(2,1)S(1)}, bf16[144,512]{1,0:T(8,128)(2,1)S(1)}, u32[]{:S(2)}, u32[]{:S(2)}) collective-permute-start(bf16[144,512]{1,0:T(8,128)(2,1)S(1)} %collective-permute-done.14.refs_1_), channel_id=1, source_target_pairs={{0,1},{1,0},{2,3},{3,2},{4,5},{5,4},{6,7},{7,6},{8,9},{9,8},{10,11... | collective-permute-start | bytes 442376 | tf_op jit(solution)/shard_map/ppermute | solution.py:53
  43.2 2.0 %collective-permute-start.7 = (bf16[256,512]{1,0:T(8,128)(2,1)S(1)}, bf16[256,512]{1,0:T(8,128)(2,1)S(1)}, u32[]{:S(2)}, u32[]{:S(2)}) collective-permute-start(bf16[256,512]{1,0:T(8,128)(2,1)S(1)} %collective-permute-done.6.refs_4_), channel_id=1, source_target_pairs={{0,1},{1,0},{2,3},{3,2},{4,5},{5,4},{6,7},{7,6},{8,9},{9,8},{10,11... | collective-permute-start | bytes 786440 | tf_op jit(solution)/shard_map/ppermute | solution.py:53
  43.5 2.1 %collective-permute-start.9 = (bf16[256,512]{1,0:T(8,128)(2,1)S(1)}, bf16[256,512]{1,0:T(8,128)(2,1)S(1)}, u32[]{:S(2)}, u32[]{:S(2)}) collective-permute-start(bf16[256,512]{1,0:T(8,128)(2,1)S(1)} %collective-permute-done.8.refs_6_), channel_id=1, source_target_pairs={{0,1},{1,0},{2,3},{3,2},{4,5},{5,4},{6,7},{7,6},{8,9},{9,8},{10,11... | collective-permute-start | bytes 786440 | tf_op jit(solution)/shard_map/ppermute | solution.py:53
  44.4 10.4 %collective-permute-start.11 = (bf16[256,512]{1,0:T(8,128)(2,1)S(1)}, bf16[256,512]{1,0:T(8,128)(2,1)S(1)}, u32[]{:S(2)}, u32[]{:S(2)}) collective-permute-start(bf16[256,512]{1,0:T(8,128)(2,1)S(1)} %collective-permute-done.10.refs_8_), channel_id=1, source_target_pairs={{0,1},{1,0},{2,3},{3,2},{4,5},{5,4},{6,7},{7,6},{8,9},{9,8},{10,11... | collective-permute-start | bytes 786440 | tf_op jit(solution)/shard_map/ppermute | solution.py:53
  45.2 11.2 %collective-permute-start.22 = (bf16[128,512]{1,0:T(8,128)(2,1)S(1)}, bf16[128,512]{1,0:T(8,128)(2,1)S(1)}, u32[]{:S(2)}, u32[]{:S(2)}) collective-permute-start(bf16[128,512]{1,0:T(8,128)(2,1)S(1)} %project.5), channel_id=1, source_target_pairs={{0,8},{1,9},{8,0},{9,1},{16,24},{17,25},{24,16},{25,17},{2,10},{3,... | collective-permute-start | bytes 393224 | tf_op jit(solution)/shard_map/ppermute | solution.py:49
  45.7 10.7 %collective-permute-start.23 = (bf16[128,512]{1,0:T(8,128)(2,1)S(1)}, bf16[128,512]{1,0:T(8,128)(2,1)S(1)}, u32[]{:S(2)}, u32[]{:S(2)}) collective-permute-start(bf16[128,512]{1,0:T(8,128)(2,1)S(1)} %project.5), channel_id=1, source_target_pairs={{0,1},{1,0},{8,16},{9,17},{16,8},{17,9},{24,25},{25,24},{2,3},{3,2... | collective-permute-start | bytes 393224 | tf_op jit(solution)/shard_map/ppermute | solution.py:49
